TPU v7x, 256 devices: a whole 4x4x8 slice. The times are simulated.
256 devices in a mesh: ga: 16 (over z_lo, y), pair: 16 (over z_hi, x, core).
Axes of the slice: x: 4, y: 4, z: 8 (z_hi: 2, z_lo: 4; z = z_hi * 4 + z_lo), core: 2. Of those that a mesh axis runs over, the one named last changes fastest.
Arguments:
- val_density: bfloat16 [256, 3, 2, 8192], P('pair', None, None, 'ga'), may hold values from -0.0625 to 0.0625
- con_density: bfloat16 [576, 3, 2, 8192], P('ga', None, None, 'pair'), may hold values from -6 to 6
- screened: bfloat16 [3, 2, 8192, 8192], P(None, None, 'ga', 'pair'), may hold values from -0.0625 to 0.0625
- coulomb: float32 [3, 8192], P(None, 'ga'), may hold values from 0.2 to 2
- trans_here: bfloat16 [384, 2, 8192], P('pair', None, 'ga'), may hold values from -6 to 6
- trans_there: bfloat16 [384, 3, 2, 8192], P('pair', None, None, 'ga'), may hold values from -0.0625 to 0.0625
- shift_map: int32 [3, 8192], P(None, 'pair'), may hold values from 0 to 8191, as said below
- ordering: int32 [384], replicated, may hold values from 0 to 383, each once
Outputs:
- kernel: float32 [3, 2, 384, 384], P(None, None, 'pair', 'ga')
Inputs may be any that keep to these rules, and one draw needn't show every extreme that they name: `shift_map`: each aligned block of 128 entries of a row is a permutation of that block's own G-vector indices.
All inputs are finite; a program needn't handle non-finite values.
Results may differ from a plain program's by a relative error of at most 0.0003.
Values may be sent and summed in bfloat16 or wider, within the bound.
A program may use at most 64 MiB of HBM per device.

v0:
```python
import jax
import jax.numpy as jnp
from jax import lax
from jax.sharding import PartitionSpec as P

NV = 16
NC = 24
GBLK = 128
NT = 384


def contract_float(left, right):
    high = lax.Precision.HIGHEST
    real_part = jnp.einsum(
        "nkg,mkg->nkm", left[:, :, 0], right[:, :, 0], precision=high
    ) - jnp.einsum("nkg,mkg->nkm", left[:, :, 1], right[:, :, 1], precision=high)
    imag_part = jnp.einsum(
        "nkg,mkg->nkm", left[:, :, 0], right[:, :, 1], precision=high
    ) + jnp.einsum("nkg,mkg->nkm", left[:, :, 1], right[:, :, 0], precision=high)
    return jnp.stack([real_part, imag_part], axis=2)


def times_cols(rows, weights):
    first = jnp.einsum(
        "nkh,kgh->nkg", rows[:, :, 0], weights[:, 0], preferred_element_type=jnp.float32
    ) - jnp.einsum("nkh,kgh->nkg", rows[:, :, 1], weights[:, 1], preferred_element_type=jnp.float32)
    second = jnp.einsum(
        "nkh,kgh->nkg", rows[:, :, 0], weights[:, 1], preferred_element_type=jnp.float32
    ) + jnp.einsum("nkh,kgh->nkg", rows[:, :, 1], weights[:, 0], preferred_element_type=jnp.float32)
    return jnp.stack([first, second], axis=2)


def on_device(
    val_density, con_density, screened, coulomb, trans_here, trans_there, shift_map, ordering
):
    con_count = con_density.shape[0]
    points = con_density.shape[1]
    slab_cols = con_density.shape[3]
    blocks = slab_cols // GBLK
    within = (shift_map % GBLK).reshape(points, blocks, GBLK)
    onehot = (
        within[:, :, :, None] == jnp.arange(GBLK, dtype=jnp.int32)[None, None, None, :]
    ).astype(jnp.bfloat16)
    con_blocks = con_density.reshape(con_count, points, 2, blocks, GBLK)
    shifted = (
        jnp.einsum("bkpnh,kngh->bkpng", con_blocks, onehot, preferred_element_type=jnp.float32)
        .astype(jnp.bfloat16)
        .reshape(con_density.shape)
    )
    whole_here = lax.all_gather(trans_here, "pair", axis=0, tiled=True).astype(jnp.float32)
    weighted = trans_there.astype(jnp.float32) * coulomb[None, :, None, :]
    high = lax.Precision.HIGHEST
    exch_real = jnp.einsum(
        "tg,skg->tks", whole_here[:, 0], weighted[:, :, 0], precision=high
    ) - jnp.einsum("tg,skg->tks", whole_here[:, 1], weighted[:, :, 1], precision=high)
    exch_imag = jnp.einsum(
        "tg,skg->tks", whole_here[:, 0], weighted[:, :, 1], precision=high
    ) + jnp.einsum("tg,skg->tks", whole_here[:, 1], weighted[:, :, 0], precision=high)
    exch_part = jnp.stack([exch_real, exch_imag], axis=2)
    whole_con = lax.all_gather(shifted, "ga", axis=0, tiled=True)
    screened_rows = lax.psum_scatter(
        times_cols(whole_con, screened), "pair", scatter_dimension=0, tiled=True
    )
    direct_part = contract_float(
        lax.all_gather(val_density, "pair", axis=0, tiled=True).astype(jnp.float32), screened_rows
    )
    direct_sum, exch_sum = lax.psum((direct_part, exch_part), "ga")
    direct_full, exch_full = (
        lax.all_gather(direct_sum, "pair", axis=3, tiled=True),
        lax.all_gather(exch_sum, "pair", axis=3, tiled=True),
    )
    row_count = NT // lax.axis_size("pair")
    col_count = NT // lax.axis_size("ga")
    row_trans = lax.dynamic_slice_in_dim(ordering, lax.axis_index("pair") * row_count, row_count, 0)
    col_trans = lax.dynamic_slice_in_dim(ordering, lax.axis_index("ga") * col_count, col_count, 0)
    row_pairs = (row_trans // NC)[:, None] * NV + (col_trans // NC)[None, :]
    col_pairs = (row_trans % NC)[:, None] * NC + (col_trans % NC)[None, :]
    picked = direct_full[row_pairs.reshape(-1)]
    col_mask = (
        col_pairs.reshape(-1)[:, None] == jnp.arange(direct_full.shape[3], dtype=jnp.int32)[None, :]
    ).astype(jnp.float32)
    direct_flat = jnp.sum(picked * col_mask[:, None, None, :], axis=3)
    direct_sel = jnp.transpose(direct_flat.reshape(row_count, col_count, points, 2), (2, 3, 0, 1))
    exch_picked = exch_full[row_trans]
    col_hot = (jnp.arange(NT, dtype=jnp.int32)[:, None] == col_trans[None, :]).astype(jnp.float32)
    exch_sel = jnp.einsum("rkpt,tc->kprc", exch_picked, col_hot, precision=high)
    return 2.0 * exch_sel - direct_sel


def solution(mesh):
    in_specs = (
        P("pair", None, None, "ga"),
        P("ga", None, None, "pair"),
        P(None, None, "ga", "pair"),
        P(None, "ga"),
        P("pair", None, "ga"),
        P("pair", None, None, "ga"),
        P(None, "pair"),
        P(),
    )
    out_specs = P(None, None, "pair", "ga")
    return jax.shard_map(
        on_device, mesh=mesh, in_specs=in_specs, out_specs=out_specs, check_vma=False
    )
```

profile of v0, /device:TPU:1, one launch (start us, length us, event | category | flops | bytes accessed | tf_op | source)
XLA Modules:
  0.0 732.0 jit_solution(17700112051085489857)
XLA Ops:
  9.8 80.6 %all-gather.7.cloned.1.call-done = bf16[576,3,2,512]{3,2,1,0:T(2,128)(2,1)} async-done(((bf16[36,3,2,512]{3,2,1,0:T(2,128)(2,1)}), bf16[576,3,2,512]{3,2,1,0:T(2,128)(2,1)}) %all-gather.7.cloned.1.call-update) | async-done | bytes 3538960 | tf_op jit(solution)/shard_map/all_gather | solution.py:60
  90.4 9.1 %fusion.34 = (bf16[576,3,1,512]{3,2,1,0:T(2,128)(2,1)S(1)}, bf16[576,3,1,512]{3,2,1,0:T(2,128)(2,1)S(1)}) fusion(bf16[576,3,2,512]{3,2,1,0:T(2,128)(2,1)} %all-gather.7.cloned.1.call-done), kind=kLoop, calls=%fused_computation.75 | loop fusion | bytes 7077888 | tf_op jit(solution)/shard_map/slice | solution.py:26
  101.8 1.2 subtract_bitcast_fusion
  102.9 1.2 add_bitcast_fusion
  104.1 3.8 pad_maximum_fusion
  107.9 11.3 %copy.40 = f32[576,3,2,512]{3,2,1,0:T(2,128)} copy(f32[576,3,2,512]{3,0,1,2:T(8,128)} %pad_maximum_fusion) | data formatting | bytes 14155776 | tf_op jit(solution)/shard_map/stack | solution.py:30
  122.2 47.9 %all_gather.15 = bf16[384,2,512]{2,0,1:T(8,128)(2,1)S(1)} all-gather(bf16[24,2,512]{2,0,1:T(8,128)(2,1)S(1)} %copy.31), channel_id=1, replica_groups=mesh['ga'=16,'pair'=16] {'pair'}, dimensions={0}, use_global_device_ids=true | all-gather | bytes 835584 | tf_op jit(solution)/shard_map/all_gather | solution.py:50
  172.8 168.5 %all-reduce.5.cloned.1.call-done = f32[576,3,2,512]{3,2,1,0:T(2,128)} async-done(((f32[576,3,2,512]{3,2,1,0:T(2,128)}), f32[576,3,2,512]{3,2,1,0:T(2,128)}) %all-reduce.5.cloned.1.call-update) | async-done | bytes 7077904
  341.3 1.5 constant_dynamic-slice_fusion
  342.8 64.9 %all-gather.9.cloned.1.call-done = bf16[256,3,2,512]{3,0,1,2:T(8,128)(2,1)} async-done(((bf16[16,3,2,512]{3,0,1,2:T(8,128)(2,1)}), bf16[256,3,2,512]{3,0,1,2:T(8,128)(2,1)}) %all-gather.9.cloned.1.call-update) | async-done | bytes 1572880 | tf_op jit(solution)/shard_map/all_gather | solution.py:65
  407.7 2.0 fusion.21
  409.7 1.9 fusion.20
  411.7 1.9 fusion.13
  415.2 146.2 %all-reduce.7.cloned.1.call-done = (f32[384,3,2,24]{0,3,1,2:T(8,128)}, f32[256,3,2,36]{0,3,1,2:T(8,128)}) async-done(((f32[384,3,2,24]{0,3,1,2:T(8,128)}, f32[256,3,2,36]{0,3,1,2:T(8,128)}), (f32[384,3,2,24]{0,3,1,2:T(8,128)}, f32[256,3,2,36]{0,3,1,2:T(8,128)})) %all-reduce.7.cloned.1.call-update) | async-done | bytes 442384 | tf_op jit(solution)/shard_map/psum | solution.py:67
  561.3 1.8 copy.44
  564.3 80.0 %all-gather.11.cloned.1.call-done = f32[256,3,2,576]{0,2,1,3:T(2,128)} async-done(((f32[256,3,2,36]{0,2,1,3:T(2,128)}), f32[256,3,2,576]{0,2,1,3:T(2,128)}) %all-gather.11.cloned.1.call-update) | async-done | bytes 3538960 | tf_op jit(solution)/shard_map/all_gather | solution.py:69
  644.3 8.0 %copy.45 = f32[256,3,2,576]{3,2,1,0:T(2,128)} copy(f32[256,3,2,576]{0,2,1,3:T(2,128)} %all-gather.11.cloned.1.call-done) | data formatting | bytes 7077888 | tf_op jit(solution)/shard_map/all_gather | solution.py:69
  652.4 25.7 %gather_fusion.1 = f32[576,3,2,576]{3,2,1,0:T(2,128)} fusion(f32[256,3,2,576]{3,2,1,0:T(2,128)} %copy.45, s32[1024]{0:T(1024)S(1)} %pad_clamp_fusion), kind=kCustom, calls=%fused_computation.1 | custom fusion | bytes 15927552 | tf_op jit(solution)/shard_map/gather | solution.py:78
  678.1 6.7 multiply_reduce_fusion
  684.8 1.2 copy.47
  686.0 29.2 %all-gather.5.cloned.1.call-done = f32[384,3,2,384]{0,3,1,2:T(8,128)} async-done(((f32[384,3,2,24]{0,3,1,2:T(8,128)}), f32[384,3,2,384]{0,3,1,2:T(8,128)}) %all-gather.5.cloned.1.call-update) | async-done | bytes 3538960 | tf_op jit(solution)/shard_map/all_gather | solution.py:70
  715.3 6.2 copy.32
  721.5 1.5 gather_fusion
  723.0 1.5 fusion.17
  (57 shorter events, 13.7 us)
Async XLA Ops:
  6.5 83.9 %all-gather.7.cloned.1.call-start = ((), (), s32[]{:S(2)}) async-start(), calls=%async_computation.1 | async-start | bytes 3760128 | tf_op jit(solution)/shard_map/all_gather | solution.py:60
  9.7 89.8 %copy-start = (bf16[3,2,512,512]{3,2,1,0:T(8,128)(2,1)S(1)}, bf16[3,2,512,512]{3,2,1,0:T(8,128)(2,1)}, u32[]{:S(2)}) copy-start(bf16[3,2,512,512]{3,2,1,0:T(8,128)(2,1)} %param.10) | copy-start | bytes 9437188
  9.7 331.5 %all-reduce.5.cloned.1.call-start = ((), (), s32[]{:S(2)}) async-start(), calls=%async_computation.4 | async-start | bytes 14155776
  119.2 0.9 copy-start.3
  119.2 1.6 copy-start.4
  119.2 1.7 copy-start.7
  119.2 2.9 copy-start.2
  119.2 2.9 copy-start.5
  119.3 288.4 %all-gather.9.cloned.1.call-start = ((), (), s32[]{:S(2)}) async-start(), calls=%async_computation.2 | async-start | bytes 1671168 | tf_op jit(solution)/shard_map/all_gather | solution.py:65
  120.8 440.5 %all-reduce.7.cloned.1.call-start = ((), (), s32[]{:S(2)}) async-start(), calls=%async_computation.5 | async-start | bytes 933888 | tf_op jit(solution)/shard_map/psum | solution.py:67
  342.8 220.9 %copy-start.6 = (s32[384]{0:T(512)S(1)}, s32[384]{0:T(512)}, u32[]{:S(2)}) copy-start(s32[384]{0:T(512)} %param.15) | copy-start | bytes 4612
  407.7 5.9 copy-start.1
  415.1 229.2 %all-gather.11.cloned.1.call-start = ((), (), s32[]{:S(2)}) async-start(), calls=%async_computation.3 | async-start | bytes 3760128 | tf_op jit(solution)/shard_map/all_gather | solution.py:69
  563.1 152.2 %all-gather.5.cloned.1.call-start = ((), (), s32[]{:S(2)}) async-start(), calls=%async_computation | async-start | bytes 3760128 | tf_op jit(solution)/shard_map/all_gather | solution.py:70
Sparse Core Ops, SparseCore 0:
  9.8 80.5 all-gather.6
  119.4 221.8 all-reduce.4
  344.1 63.5 all-gather.8
  415.2 146.0 all-reduce.6
  563.9 80.4 all-gather.10
  646.9 68.3 all-gather.4
where the time goes:
time: 733 us; the launch traced here: 732 us
  waiting for transfers between devices  570 us (78%)
  local copies, waits for them, and re-layouts  71.3 us (10%)
  blocking collectives  47.9 us (7%)
  matrix products  15.1 us (2%)
  between operations  14.4 us (2%)
  other arithmetic  13 us (2%)
    unnamed x7, waiting for transfers between devices  169 us
    psum x1, waiting for transfers between devices, on_device(): direct_sum, exch_sum = lax.psum((direct_part, exch_part), 'ga')  146 us
    all_gather x1, waiting for transfers between devices, on_device(): whole_con = lax.all_gather(shifted, 'ga', axis=0, tiled=True)  80.6 us
    all_gather x1, waiting for transfers between devices, on_device(): lax.all_gather(direct_sum, 'pair', axis=3, tiled=True)  80 us
    all_gather x1, waiting for transfers between devices, on_device(): lax.all_gather(val_density, 'pair', axis=0, tiled=True).astype(jnp.float32)  64.9 us
    all_gather x1, blocking collectives, on_device(): lax.all_gather(trans_here, 'pair', axis=0, tiled=True).astype(jnp.float32)  47.9 us
    all_gather x1, waiting for transfers between devices, on_device(): lax.all_gather(exch_sum, 'pair', axis=3, tiled=True)  29.2 us
    gather x1, local copies, waits for them, and re-layouts, on_device(): picked = direct_full[row_pairs.reshape(-1)]  25.7 us
  transfers between devices with their start and end apart: 6, of which 6 were waited for; matrix products, arithmetic and copies ran while one was open for 7% of the time, Pallas kernels for 0%

commit v1 on v0

v1 whole, which is shorter than its diff:
```python
import jax
import jax.numpy as jnp
from jax import lax
from jax.sharding import PartitionSpec as P

NV = 16
NC = 24
GBLK = 128
NT = 384
F32 = jnp.float32
BF16 = jnp.bfloat16


def two_terms(values):
    high = lax.reduce_precision(values, exponent_bits=8, mantissa_bits=7)
    low = lax.reduce_precision(values - high, exponent_bits=8, mantissa_bits=7)
    return high.astype(BF16), low.astype(BF16)


def on_device(
    val_density, con_density, screened, coulomb, trans_here, trans_there, shift_map, ordering
):
    con_count, points, _, slab_cols = con_density.shape
    blocks = slab_cols // GBLK
    pairs = lax.axis_size("pair")
    slabs = lax.axis_size("ga")
    whole_con = lax.all_gather(con_density, "ga", axis=0, tiled=True)
    whole_val = lax.all_gather(val_density, "pair", axis=0, tiled=True)
    whole_here = lax.all_gather(trans_here, "pair", axis=0, tiled=True)
    within = (shift_map % GBLK).reshape(points, blocks, GBLK)
    onehot = (
        within[:, :, :, None] == jnp.arange(GBLK, dtype=jnp.int32)[None, None, None, :]
    ).astype(BF16)

    def mul(spec, left, right):
        return jnp.einsum(spec, left, right, preferred_element_type=F32)

    rows_re = mul("akg,kgh->kah", whole_val[:, :, 0], screened[:, 0]) - mul(
        "akg,kgh->kah", whole_val[:, :, 1], screened[:, 1]
    )
    rows_im = mul("akg,kgh->kah", whole_val[:, :, 0], screened[:, 1]) + mul(
        "akg,kgh->kah", whole_val[:, :, 1], screened[:, 0]
    )
    shape = (points, NV * NV, blocks, GBLK)

    def unshift(term):
        moved = mul("kang,kngh->kanh", term.reshape(shape), onehot).astype(BF16)
        return moved.reshape(points, NV * NV, slab_cols)

    real = [unshift(term) for term in two_terms(rows_re)]
    imag = [unshift(term) for term in two_terms(rows_im)]
    left_re = jnp.concatenate([real[0], -imag[0], real[1], -imag[1]], axis=2)
    left_im = jnp.concatenate([imag[0], real[0], imag[1], real[1]], axis=2)
    con_rows = jnp.transpose(whole_con, (1, 0, 2, 3)).reshape(points, NC * NC, 2 * slab_cols)
    con_twice = jnp.concatenate([con_rows, con_rows], axis=2)
    direct = jnp.stack(
        [mul("kax,kbx->kab", left_re, con_twice), mul("kax,kbx->kab", left_im, con_twice)], axis=1
    )
    direct = jnp.transpose(direct.reshape(points, 2, NV, NV, NC * NC), (3, 0, 1, 2, 4))
    direct = lax.psum_scatter(direct, "pair", scatter_dimension=0, tiled=True)[0]
    direct = jnp.transpose(direct.reshape(points, 2, NV, NC, NC), (2, 3, 0, 1, 4)).reshape(
        NT, points, 2, NC
    )
    weighted = trans_there.astype(F32) * coulomb[None, :, None, :]
    high = lax.Precision.HIGHEST
    here = whole_here.astype(F32)
    exch_re = jnp.einsum("tg,skg->tks", here[:, 0], weighted[:, :, 0], precision=high) - jnp.einsum(
        "tg,skg->tks", here[:, 1], weighted[:, :, 1], precision=high
    )
    exch_im = jnp.einsum("tg,skg->tks", here[:, 0], weighted[:, :, 1], precision=high) + jnp.einsum(
        "tg,skg->tks", here[:, 1], weighted[:, :, 0], precision=high
    )
    natural = 2.0 * jnp.stack([exch_re, exch_im], axis=2) - direct
    rows = natural[ordering]
    rows = lax.all_to_all(
        rows.reshape(pairs, NT // pairs, points, 2, NC), "pair", split_axis=0, concat_axis=0
    )
    cols = jnp.transpose(rows, (0, 4, 2, 3, 1)).reshape(NT, points * 2 * (NT // pairs))
    cols = cols[ordering]
    cols = lax.psum_scatter(cols, "ga", scatter_dimension=0, tiled=True)
    cols = cols.reshape(NT // slabs, points, 2, NT // pairs)
    return jnp.transpose(cols, (1, 2, 3, 0))


def solution(mesh):
    in_specs = (
        P("pair", None, None, "ga"),
        P("ga", None, None, "pair"),
        P(None, None, "ga", "pair"),
        P(None, "ga"),
        P("pair", None, "ga"),
        P("pair", None, None, "ga"),
        P(None, "pair"),
        P(),
    )
    out_specs = P(None, None, "pair", "ga")
    return jax.shard_map(
        on_device, mesh=mesh, in_specs=in_specs, out_specs=out_specs, check_vma=False
    )
```

time: 733 us -> 405 us (0.55)
  the two profiles are of different devices: /device:TPU:1 before, /device:TPU:2 now
where the time goes in v1:
time: 405 us
  waiting for transfers between devices  285 us (70%)
  blocking collectives  39.9 us (10%)
  local copies, waits for them, and re-layouts  39.7 us (10%)
  matrix products  21.6 us (5%)
  between operations  13.5 us (3%)
  other arithmetic  4.33 us (1%)
    reduce_scatter x1, waiting for transfers between devices, on_device(): cols = lax.psum_scatter(cols, 'ga', scatter_dimension=0, tiled=True)  85.2 us
    reduce_scatter x1, waiting for transfers between devices, on_device(): lax.psum_scatter(direct, 'pair', scatter_dimension=0, tiled=True)[0]  70.6 us
    all_gather x1, waiting for transfers between devices, on_device(): whole_con = lax.all_gather(con_density, 'ga', axis=0, tiled=True)  66.7 us
    all_gather x1, waiting for transfers between devices, on_device(): whole_val = lax.all_gather(val_density, 'pair', axis=0, tiled=True)  62.1 us
    all_gather x1, blocking collectives, on_device(): whole_here = lax.all_gather(trans_here, 'pair', axis=0, tiled=True)  26.4 us
    dot_general x10, matrix products, mul(): return jnp.einsum(spec, left, right, preferred_element_type=F32)  19.7 us
    all_to_all x1, blocking collectives, on_device(): lax.all_to_all(rows.reshape(pairs, NT // pairs, points, 2, NC), 'pair', s...  13.5 us
  transfers between devices with their start and end apart: 4, of which 4 were waited for; matrix products, arithmetic and copies ran while one was open for 5% of the time, Pallas kernels for 0%

profile of v1, /device:TPU:2, one launch (start us, length us, event | category | flops | bytes accessed | tf_op | source)
XLA Modules:
  0.0 404.5 jit_solution(9876181623509086774)
XLA Ops:
  6.5 1.7 copy.57
  9.8 62.1 %all-gather.3.cloned.1.call-done = bf16[256,3,2,512]{3,0,1,2:T(8,128)(2,1)} async-done(((bf16[16,3,2,512]{3,0,1,2:T(8,128)(2,1)}), bf16[256,3,2,512]{3,0,1,2:T(8,128)(2,1)}) %all-gather.3.cloned.1.call-update) | async-done | bytes 1572880 | tf_op jit(solution)/shard_map/all_gather | solution.py:28
  71.9 2.2 fusion.22
  74.1 2.7 fusion.42
  76.8 1.3 convolution_convert_fusion.1
  78.1 2.3 copy.67
  80.4 1.9 fusion.20
  82.3 1.5 fusion.43
  85.3 1.2 copy.66
  89.4 66.7 %all-gather.5.cloned.1.call-done = bf16[576,3,2,512]{3,2,1,0:T(2,128)(2,1)} async-done(((bf16[36,3,2,512]{3,2,1,0:T(2,128)(2,1)}), bf16[576,3,2,512]{3,2,1,0:T(2,128)(2,1)}) %all-gather.5.cloned.1.call-update) | async-done | bytes 3538960 | tf_op jit(solution)/shard_map/all_gather | solution.py:27
  156.1 6.2 %copy.68 = bf16[3,576,2,512]{3,2,1,0:T(2,128)(2,1)} copy(bf16[3,576,2,512]{3,2,0,1:T(2,128)(2,1)} %bitcast.118) | data formatting | bytes 7077888 | tf_op jit(solution)/shard_map/transpose | solution.py:54
  162.4 7.8 %reshape.54 = bf16[3,576,1024]{2,1,0:T(8,128)(2,1)S(1)} reshape(bf16[3,576,2,512]{3,2,1,0:T(2,128)(2,1)} %copy.68) | data formatting | bytes 7077888 | tf_op jit(solution)/shard_map/reshape | solution.py:54
  172.1 6.3 %fusion.8 = f32[3,256,576]{2,1,0:T(8,128)S(1)} fusion(bf16[3,576,2048]{2,1,0:T(8,128)(2,1)S(1)} %constant_dynamic-update-slice_fusion, bf16[3,256,512]{2,1,0:T(8,128)(2,1)} %copy.67, bf16[3,256,512]{2,1,0:T(8,128)(2,1)S(1)} %copy-done.3, bf16[3,256,512]{2,1,0:T(8,128)(2,1)} %copy.66, bf16[3,256,512]{2,1,0:T(8,128)(2,1)S(1)} %copy-done.5), kind=kOutput, calls=%fused_computation.11 | convolution fusion | flops 1824522240 | bytes 11993088 | tf_op jit(solution)/shard_map/kax,kbx->kab/dot_general | solution.py:36
  178.5 2.6 fusion
  181.4 3.1 copy.75
  185.4 26.4 %all_gather.9 = bf16[384,2,512]{2,0,1:T(8,128)(2,1)S(1)} all-gather(bf16[24,2,512]{2,0,1:T(8,128)(2,1)S(1)} %copy.56), channel_id=1, replica_groups=mesh['ga'=16,'pair'=16] {'pair'}, dimensions={0}, use_global_device_ids=true | all-gather | bytes 835584 | tf_op jit(solution)/shard_map/all_gather | solution.py:29
  213.8 70.6 %reduce-scatter.3.cloned.1.call-done = f32[1,3,2,16,576]{4,3,2,1,0:T(8,128)} async-done(((f32[16,3,2,16,576]{4,3,2,1,0:T(8,128)}), f32[1,3,2,16,576]{4,3,2,1,0:T(8,128)}) %reduce-scatter.3.cloned.1.call-update) | async-done | bytes 221200 | tf_op jit(solution)/shard_map/reduce_scatter | solution.py:60
  284.4 1.4 reshape_squeeze.3
  287.2 3.3 gather_fusion
  291.6 13.5 %all_to_all.5 = f32[16,1,3456]{2,1,0:T(1,128)S(1)} all-to-all(f32[16,1,3456]{2,1,0:T(1,128)S(1)} %reshape.80), channel_id=1, replica_groups=mesh['ga'=16,'pair'=16] {'pair'}, dimensions={0} | all-to-all | bytes 442368 | tf_op jit(solution)/shard_map/all_to_all | solution.py:75
  305.6 1.2 reduce
  309.1 2.2 gather_fusion.1
  311.3 85.2 %reduce-scatter.5.cloned.1.call-done = f32[24,144]{1,0:T(8,128)} async-done(((f32[384,144]{1,0:T(8,128)}), f32[24,144]{1,0:T(8,128)}) %reduce-scatter.5.cloned.1.call-update) | async-done | bytes 13840 | tf_op jit(solution)/shard_map/reduce_scatter | solution.py:80
  396.5 1.5 copy.86
  (70 shorter events, 16.1 us)
Async XLA Ops:
  6.5 67.6 %copy-start = (bf16[3,2,512,512]{3,2,1,0:T(8,128)(2,1)S(1)}, bf16[3,2,512,512]{3,2,1,0:T(8,128)(2,1)}, u32[]{:S(2)}) copy-start(bf16[3,2,512,512]{3,2,1,0:T(8,128)(2,1)} %param.10) | copy-start | bytes 9437188
  6.5 65.3 %all-gather.3.cloned.1.call-start = ((), (), s32[]{:S(2)}) async-start(), calls=%async_computation.3 | async-start | bytes 1671168 | tf_op jit(solution)/shard_map/all_gather | solution.py:28
  8.3 147.9 %all-gather.5.cloned.1.call-start = ((), (), s32[]{:S(2)}) async-start(), calls=%async_computation.4 | async-start | bytes 3760128 | tf_op jit(solution)/shard_map/all_gather | solution.py:27
  9.0 275.4 %reduce-scatter.3.cloned.1.call-start = ((), (), s32[]{:S(2)}) async-start(), calls=%async_computation.5 | async-start | bytes 4177920 | tf_op jit(solution)/shard_map/reduce_scatter | solution.py:60
  80.4 1.9 copy-start.1
  83.8 1.1 copy-start.6
  83.8 2.8 copy-start.7
  84.5 2.7 copy-start.2
  87.2 68.9 %copy-start.4 = (bf16[3,256,512]{2,1,0:T(8,128)(2,1)}, bf16[3,256,512]{2,1,0:T(8,128)(2,1)S(1)}, u32[]{:S(2)}) copy-start(bf16[3,256,512]{2,1,0:T(8,128)(2,1)S(1)} %copy.62) | copy-start | bytes 2359300
  170.7 1.1 copy-start.3
  170.7 1.4 copy-start.5
  172.1 6.4 %copy-start.8 = (bf16[3,256,512]{2,1,0:T(8,128)(2,1)S(1)}, bf16[3,256,512]{2,1,0:T(8,128)(2,1)}, u32[]{:S(2)}) copy-start(bf16[3,256,512]{2,1,0:T(8,128)(2,1)} %copy.67) | copy-start | bytes 2359300
  172.1 6.4 %copy-start.9 = (bf16[3,256,512]{2,1,0:T(8,128)(2,1)S(1)}, bf16[3,256,512]{2,1,0:T(8,128)(2,1)}, u32[]{:S(2)}) copy-start(bf16[3,256,512]{2,1,0:T(8,128)(2,1)} %copy.66) | copy-start | bytes 2359300
  172.1 6.4 %copy-start.10 = (bf16[3,256,512]{2,1,0:T(8,128)(2,1)S(1)}, bf16[3,256,512]{2,1,0:T(8,128)(2,1)}, u32[]{:S(2)}) copy-start(bf16[3,256,512]{2,1,0:T(8,128)(2,1)} %neg.7) | copy-start | bytes 2359300
  172.1 6.4 %copy-start.11 = (bf16[3,256,512]{2,1,0:T(8,128)(2,1)S(1)}, bf16[3,256,512]{2,1,0:T(8,128)(2,1)}, u32[]{:S(2)}) copy-start(bf16[3,256,512]{2,1,0:T(8,128)(2,1)} %neg.6) | copy-start | bytes 2359300
  184.4 0.8 copy-start.13
  184.4 0.8 copy-start.15
  184.4 1.0 copy-start.12
  184.4 1.0 copy-start.14
  184.5 212.1 %reduce-scatter.5.cloned.1.call-start = ((), (), s32[]{:S(2)}) async-start(), calls=%async_computation.6 | async-start | bytes 417792 | tf_op jit(solution)/shard_map/reduce_scatter | solution.py:80
Sparse Core Ops, SparseCore 0:
  10.1 61.7 all-gather.2
  73.7 82.4 all-gather.4
  184.6 99.7 reduce-scatter.2
  311.4 85.0 reduce-scatter.4

commit v2 on v1

v2 whole, which is shorter than its diff:
```python
import functools

import jax
import jax.numpy as jnp
from jax import lax
from jax.experimental import pallas as pl
from jax.experimental.pallas import tpu as pltpu
from jax.sharding import PartitionSpec as P

NV = 16
NC = 24
GBLK = 128
NT = 384
KSEL = 3
F32 = jnp.float32
BF16 = jnp.bfloat16
MESH = pl.DeviceIdType.MESH


def position():
    ga, pair = lax.axis_index("ga"), lax.axis_index("pair")
    return dict(
        ga=ga,
        pair=pair,
        zl=lax.div(ga, 4),
        y=lax.rem(ga, 4),
        zh=lax.div(pair, 8),
        x=lax.rem(lax.div(pair, 2), 4),
        core=lax.rem(pair, 2),
    )


def device(at, **moved):
    here = {**at, **moved}
    return (here["zl"] * 4 + here["y"], here["zh"] * 8 + here["x"] * 2 + here["core"])


def greet(peers):
    barrier = pltpu.get_barrier_semaphore()
    for peer in peers:
        pl.semaphore_signal(barrier, inc=1, device_id=peer, device_id_type=MESH)
    pl.semaphore_wait(barrier, len(peers))


def remote(src, dst, send_sem, recv_sem, to):
    return pltpu.make_async_remote_copy(
        src_ref=src, dst_ref=dst, send_sem=send_sem, recv_sem=recv_sem, device_id=to, device_id_type=MESH
    )


def dot(left, right):
    return jnp.dot(left, right, preferred_element_type=F32)


def dot_rows(left, right):
    return lax.dot_general(left, right, (((1,), (1,)), ((), ())), preferred_element_type=F32)


def two_terms(values):
    high = values.astype(BF16)
    return high, (values - high.astype(F32)).astype(BF16)


def tiles_kernel(
    con_in, val_in, here_in, scr_in, there_ref, coul_ref, within_ref,
    part_ref, exch_ref,
    con_all, val_all, here_all, weights, con_rows, left_hi, left_lo, direct, from_core, from_x,
    con_send, con_recv, val_send, val_recv, here_send, here_recv,
    core_send, core_recv, x_send, x_recv, local,
):
    at = position()
    ga, pair, zl, y, zh, x, core = (at[k] for k in ("ga", "pair", "zl", "y", "zh", "x", "core"))
    turn = lambda v, d: lax.rem(v + d, 4)
    other_core = device(at, core=1 - core)
    other_zh = device(at, zh=1 - zh)
    x_peers = [device(at, x=turn(x, d)) for d in (1, 2, 3)]
    z_peers = [device(at, zl=turn(zl, d)) for d in (1, 2, 3)]
    y_next, y_prev = device(at, y=turn(y, 1)), device(at, y=turn(y, 3))

    loads = [pltpu.make_async_copy(scr_in.at[q], weights.at[q], local.at[q]) for q in range(KSEL)]
    loads.append(pltpu.make_async_copy(val_in, val_all.at[pair], local.at[3]))
    loads.append(pltpu.make_async_copy(here_in, here_all.at[pair], local.at[4]))
    loads.append(pltpu.make_async_copy(con_in, con_all.at[ga], local.at[5]))
    for load in loads:
        load.start()
    greet([other_core, other_zh, y_next, y_prev] + x_peers + z_peers)

    pending = []

    def start(copy):
        copy.start()
        pending.append(copy)

    counts = {"con": 0, "val": 0, "here": 0}
    kinds = {
        "val": (val_in, val_all, val_send, val_recv),
        "here": (here_in, here_all, here_send, here_recv),
    }

    def send_pair(kind, owner, to, fresh):
        own, slots, send_sems, recv_sems = kinds[kind]
        src = own if fresh else slots.at[owner]
        start(remote(src, slots.at[owner], send_sems.at[counts[kind]], recv_sems.at[owner], to))
        counts[kind] += 1

    def wait_pair(kind, owner):
        own, slots, send_sems, recv_sems = kinds[kind]
        remote(own, slots.at[owner], send_sems.at[0], recv_sems.at[owner], other_core).wait_recv()

    def send_con(q, owner, to, fresh):
        src = con_in.at[q] if fresh else con_all.at[owner, q]
        start(remote(src, con_all.at[owner, q], con_send.at[counts["con"]], con_recv.at[owner, q], to))
        counts["con"] += 1

    def wait_con(q, owner):
        remote(con_in.at[q], con_all.at[owner, q], con_send.at[0], con_recv.at[owner, q], other_core).wait_recv()

    def pair_at(zh_, x_, core_):
        return zh_ * 8 + x_ * 2 + core_

    def spread_own(kind):
        send_pair(kind, pair, other_zh, True)
        for peer in x_peers:
            send_pair(kind, pair, peer, True)
        send_pair(kind, pair, other_core, True)

    def spread_rest(kind):
        owner = pair_at(1 - zh, x, core)
        wait_pair(kind, owner)
        for peer in x_peers:
            send_pair(kind, owner, peer, False)
        send_pair(kind, owner, other_core, False)
        for zh_ in (zh, 1 - zh):
            for d in (1, 2, 3):
                owner = pair_at(zh_, turn(x, d), core)
                wait_pair(kind, owner)
                send_pair(kind, owner, other_core, False)

    def gather_rest(kind):
        for zh_ in (zh, 1 - zh):
            for d in (0, 1, 2, 3):
                wait_pair(kind, pair_at(zh_, turn(x, d), 1 - core))

    def con_z(q):
        for peer in z_peers:
            send_con(q, ga, peer, True)

    def con_y(q):
        send_con(q, ga, y_next, True)
        send_con(q, ga, y_prev, True)

    def con_from_z(q):
        for d in (1, 3, 2):
            owner = turn(zl, d) * 4 + y
            wait_con(q, owner)
            send_con(q, owner, y_next, False)
            send_con(q, owner, y_prev, False)

    def con_from_y(q):
        for zl_ in (0, 1):
            owner = zl_ * 4 + turn(y, 3)
            wait_con(q, owner)
            send_con(q, owner, y_next, False)
        for zl_ in (2, 3):
            owner = zl_ * 4 + turn(y, 1)
            wait_con(q, owner)
            send_con(q, owner, y_prev, False)

    def con_rest(q):
        for zl_ in (2, 3):
            wait_con(q, zl_ * 4 + turn(y, 3))
        for zl_ in (0, 1):
            wait_con(q, zl_ * 4 + turn(y, 1))
        for zl_ in (0, 1, 2, 3):
            wait_con(q, zl_ * 4 + turn(y, 2))

    def unshift_weights(q):
        loads[q].wait()
        for n in range(4):
            row = within_ref[pl.ds(q * 4 + n, 1), :]
            onehot = (lax.broadcasted_iota(jnp.int32, (GBLK, GBLK), 0) == row).astype(F32).astype(BF16)
            cols = slice(n * GBLK, (n + 1) * GBLK)
            weights[q, :, cols] = dot_rows(weights[q, :, cols], onehot).astype(BF16)

    def rows_of(q):
        to_row = lax.broadcasted_iota(jnp.int32, (NV * NV, NV * NV), 0)
        from_row = lax.broadcasted_iota(jnp.int32, (NV * NV, NV * NV), 1)
        v, place = to_row & 15, to_row >> 4
        w = (place & 1) * 8 + ((place >> 1) & 3) * 2 + (place >> 3)
        order = (from_row == v * NV + w).astype(F32).astype(BF16)
        gathered = val_all[:, q].reshape(NV * NV, 1024)
        val = dot(order, gathered).astype(BF16)
        val_re, val_im = val[:, :512], val[:, 512:]
        scr_re, scr_im = weights[q, :512, :], weights[q, 512:, :]
        real_hi, real_lo = two_terms(dot(val_re, scr_re) - dot(val_im, scr_im))
        imag_hi, imag_lo = two_terms(dot(val_re, scr_im) + dot(val_im, scr_re))
        for ref, real, imag in ((left_hi, real_hi, imag_hi), (left_lo, real_lo, imag_lo)):
            ref[q, 0, :, :512] = real
            ref[q, 0, :, 512:] = -imag
            ref[q, 1, :, :512] = imag
            ref[q, 1, :, 512:] = real

    def contract(q):
        con_rest(q)
        for owner in range(16):
            con_rows[owner * 36 : (owner + 1) * 36, :] = con_all[owner, q]

        @pl.loop(0, 2)
        def _(p):
            direct[q, p] = dot_rows(left_hi[q, p], con_rows[...]) + dot_rows(left_lo[q, p], con_rows[...])

        start(
            remote(
                direct.at[q, :, pl.ds(pl.multiple_of((1 - core) * 128, 128), 128), :],
                from_core.at[q], core_send.at[q], core_recv.at[q], other_core,
            )
        )

    def add_core(q):
        own = pl.ds(pl.multiple_of(core * 128, 128), 128)
        remote(direct.at[q, :, own, :], from_core.at[q], core_send.at[q], core_recv.at[q], other_core).wait_recv()
        for p in range(2):
            direct[q, p, own, :] = direct[q, p, own, :] + from_core[q, p]
        for d in (1, 2, 3):
            rows = pl.ds(pl.multiple_of(core * 128 + turn(x, d) * 32, 32), 32)
            start(
                remote(
                    direct.at[q, :, rows, :], from_x.at[q, d - 1],
                    x_send.at[q, d - 1], x_recv.at[q, d - 1], x_peers[d - 1],
                )
            )

    def add_x(q):
        rows = pl.ds(pl.multiple_of(core * 128 + x * 32, 32), 32)
        for d in (1, 2, 3):
            remote(
                direct.at[q, :, rows, :], from_x.at[q, d - 1],
                x_send.at[q, d - 1], x_recv.at[q, d - 1], x_peers[d - 1],
            ).wait_recv()
        for p in range(2):
            part_ref[q, p] = direct[q, p, rows, :] + from_x[q, 0, p] + from_x[q, 1, p] + from_x[q, 2, p]

    def exchange():
        gather_rest("here")
        loads[4].wait()
        terms = []
        for q in range(KSEL):
            values = there_ref[q].astype(F32) * coul_ref[pl.ds(q, 1), :]
            high, low = two_terms(values)
            for p in range(2):
                for term in (high, low):
                    if p == 0:
                        swapped = jnp.concatenate([term[:, :512], -term[:, 512:]], axis=1)
                    else:
                        swapped = jnp.concatenate([term[:, 512:], term[:, :512]], axis=1)
                    terms.append(swapped)
        highs = jnp.concatenate([t.astype(F32) for t in terms[0::2]], axis=0).astype(BF16)
        lows = jnp.concatenate([t.astype(F32) for t in terms[1::2]], axis=0).astype(BF16)
        for v in range(NV):
            rows = here_all[v]
            exch_ref[v * NC : (v + 1) * NC, :] = dot_rows(rows, highs) + dot_rows(rows, lows)

    spread_own("val")
    con_z(0)
    con_y(0)
    spread_own("here")
    con_z(1)
    con_z(2)
    con_y(1)
    for q in range(KSEL):
        unshift_weights(q)
    spread_rest("val")
    con_from_z(0)
    gather_rest("val")
    loads[3].wait()
    rows_of(0)
    loads[5].wait()
    con_from_y(0)
    con_y(2)
    con_from_z(1)
    spread_rest("here")
    rows_of(1)
    contract(0)
    con_from_y(1)
    con_from_z(2)
    rows_of(2)
    add_core(0)
    contract(1)
    con_from_y(2)
    exchange()
    add_core(1)
    contract(2)
    add_x(0)
    add_core(2)
    add_x(1)
    add_x(2)
    for copy in pending:
        copy.wait_send()


def gather_and_multiply(con, val, here, scr, there, coul, within):
    any_space = pl.BlockSpec(memory_space=pl.ANY)
    vmem = pl.BlockSpec(memory_space=pltpu.VMEM)
    dma = pltpu.SemaphoreType.DMA
    return pl.pallas_call(
        tiles_kernel,
        name="gather_and_multiply",
        out_shape=(
            jax.ShapeDtypeStruct((KSEL, 2, 32, NC * NC), F32),
            jax.ShapeDtypeStruct((NT, KSEL * 2 * NC), F32),
        ),
        in_specs=[any_space] * 4 + [vmem] * 3,
        out_specs=(vmem, vmem),
        scratch_shapes=[
            pltpu.VMEM((16, KSEL, 36, 1024), BF16),
            pltpu.VMEM((16, KSEL, NV, 1024), BF16),
            pltpu.VMEM((16, NC, 1024), BF16),
            pltpu.VMEM((KSEL, 1024, 512), BF16),
            pltpu.VMEM((NC * NC, 1024), BF16),
            pltpu.VMEM((KSEL, 2, NV * NV, 1024), BF16),
            pltpu.VMEM((KSEL, 2, NV * NV, 1024), BF16),
            pltpu.VMEM((KSEL, 2, NV * NV, NC * NC), F32),
            pltpu.VMEM((KSEL, 2, 128, NC * NC), F32),
            pltpu.VMEM((KSEL, 3, 2, 32, NC * NC), F32),
            dma((45,)), dma((16, KSEL)), dma((16,)), dma((16,)), dma((16,)), dma((16,)),
            dma((KSEL,)), dma((KSEL,)), dma((KSEL, 3)), dma((KSEL, 3)), dma((6,)),
        ],
        compiler_params=pltpu.CompilerParams(
            collective_id=0, has_side_effects=True, vmem_limit_bytes=60 * 2**20
        ),
    )(con, val, here, scr, there, coul, within)


def order_kernel(
    part_ref, exch_ref, places_ref, out_ref,
    rows_all, moved, from_x, whole, cols, from_y, slab, from_z,
    x_send, x_recv, y_send, y_recv, z_send, z_recv,
):
    at = position()
    ga, pair, zl, y, zh, x, core = (at[k] for k in ("ga", "pair", "zl", "y", "zh", "x", "core"))
    turn = lambda v, d: lax.rem(v + d, 4)
    z = zh * 4 + zl
    x_steps = [(d, c) for c in (0, 1) for d in range(4) if (d, c) != (0, 0)]
    x_peers = [device(at, x=turn(x, d), core=lax.rem(core + c, 2)) for d, c in x_steps]
    y_peers = [device(at, y=turn(y, d)) for d in (1, 2, 3)]
    z_to = [lax.rem(z + d, 8) for d in range(1, 8)]
    z_peers = [device(at, zh=lax.div(t, 4), zl=lax.rem(t, 4)) for t in z_to]
    greet(x_peers + y_peers + z_peers)
    pending = []

    def start(copy):
        copy.start()
        pending.append(copy)

    places = jnp.transpose(jnp.broadcast_to(places_ref[...].astype(F32), (GBLK, NT)))
    lanes = lax.broadcasted_iota(jnp.int32, (NT, GBLK), 1)
    natural, swapped = [], []
    whole_places = places.astype(jnp.int32)
    band = jnp.zeros((NT, GBLK), jnp.int32)
    for step in range(1, NV):
        band = band + (whole_places >= step * NC).astype(jnp.int32)
    other = (whole_places - band * NC) * NV + band
    for n in range(3):
        natural.append((whole_places == lanes + n * GBLK).astype(F32))
        swapped.append((other == lanes + n * GBLK).astype(F32))
    natural = jnp.concatenate(natural, axis=1).astype(BF16)
    swapped = jnp.concatenate(swapped, axis=1).astype(BF16)

    for half in range(2):
        for q in range(KSEL):
            for p in range(2):
                tile = part_ref[q, p, half * NV : (half + 1) * NV, :]
                lane = half * 144 + (q * 2 + p) * NC
                for c in range(NC):
                    rows_all[c * NV : (c + 1) * NV, lane : lane + NC] = tile[:, c * NC : (c + 1) * NC]
    rows_hi, rows_lo = two_terms(rows_all[...])
    exch_hi, exch_lo = two_terms(exch_ref[...])
    exch = 2.0 * (dot(natural, exch_hi) + dot(natural, exch_lo))
    direct = dot(swapped, rows_hi) + dot(swapped, rows_lo)
    mine = zh.astype(F32)
    moved[:, 0:144] = exch * (1.0 - mine) - direct[:, 0:144]
    moved[:, 144:288] = exch * mine - direct[:, 144:288]

    def row_block(zh_, x_, core_):
        return pl.ds(pl.multiple_of((zh_ * 8 + x_ * 2 + core_) * NC, 8), NC)

    for k, (d, c) in enumerate(x_steps):
        x_, core_ = turn(x, d), lax.rem(core + c, 2)
        for half in range(2):
            start(
                remote(
                    moved.at[row_block(half, x_, core_), :], from_x.at[x * 2 + core, half],
                    x_send.at[k, half], x_recv.at[x * 2 + core, half], x_peers[k],
                )
            )
    for half in range(2):
        from_x[x * 2 + core, half] = moved[row_block(half, x, core), :]
    for k, (d, c) in enumerate(x_steps):
        slot = turn(x, d) * 2 + lax.rem(core + c, 2)
        for half in range(2):
            remote(
                from_x.at[slot, half], from_x.at[slot, half],
                x_send.at[0, half], x_recv.at[slot, half], x_peers[k],
            ).wait_recv()
    for half in range(2):
        for slot in range(8):
            tile = from_x[slot, half]
            for zh_ in range(2):
                w = zh_ * 8 + slot
                for plane in range(6):
                    lane = zh_ * 144 + plane * NC
                    whole[half, plane * NC : (plane + 1) * NC, w * NC : (w + 1) * NC] = tile[:, lane : lane + NC]
        whole_hi, whole_lo = two_terms(whole[half])
        cols[half] = dot_rows(natural, whole_hi) + dot_rows(natural, whole_lo)

    def col_block(zl_, y_):
        return pl.ds(pl.multiple_of((zl_ * 4 + y_) * NC, 8), NC)

    for d in (1, 2, 3):
        for zl_ in range(4):
            start(
                remote(
                    cols.at[:, col_block(zl_, turn(y, d)), :], from_y.at[d - 1, zl_],
                    y_send.at[d - 1, zl_], y_recv.at[d - 1, zl_], y_peers[d - 1],
                )
            )
    for zl_ in range(4):
        for d in (1, 2, 3):
            remote(
                from_y.at[d - 1, zl_], from_y.at[d - 1, zl_],
                y_send.at[d - 1, zl_], y_recv.at[d - 1, zl_], y_peers[d - 1],
            ).wait_recv()
        slab[zl_] = cols[:, col_block(zl_, y), :] + from_y[0, zl_] + from_y[1, zl_] + from_y[2, zl_]
    for d in range(1, 8):
        t = z_to[d - 1]
        start(
            remote(
                slab.at[lax.rem(t, 4), lax.div(t, 4)], from_z.at[d - 1],
                z_send.at[d - 1], z_recv.at[d - 1], z_peers[d - 1],
            )
        )
    for d in range(1, 8):
        remote(
            from_z.at[d - 1], from_z.at[d - 1], z_send.at[d - 1], z_recv.at[d - 1], z_peers[d - 1]
        ).wait_recv()
    total = slab[zl, zh]
    for d in range(7):
        total = total + from_z[d]
    out_ref[...] = total
    for copy in pending:
        copy.wait_send()


def permute_and_sum(part, exch, places):
    vmem = pl.BlockSpec(memory_space=pltpu.VMEM)
    dma = pltpu.SemaphoreType.DMA
    return pl.pallas_call(
        order_kernel,
        name="permute_and_sum",
        out_shape=jax.ShapeDtypeStruct((NC, KSEL * 2 * NC), F32),
        in_specs=[vmem] * 3,
        out_specs=vmem,
        scratch_shapes=[
            pltpu.VMEM((NT, 288), F32),
            pltpu.VMEM((NT, 288), F32),
            pltpu.VMEM((8, 2, NC, 288), F32),
            pltpu.VMEM((2, 144, NT), F32),
            pltpu.VMEM((2, NT, 144), F32),
            pltpu.VMEM((3, 4, 2, NC, 144), F32),
            pltpu.VMEM((4, 2, NC, 144), F32),
            pltpu.VMEM((7, NC, 144), F32),
            dma((7, 2)), dma((8, 2)), dma((3, 4)), dma((3, 4)), dma((7,)), dma((7,)),
        ],
        compiler_params=pltpu.CompilerParams(
            collective_id=1, has_side_effects=True, vmem_limit_bytes=40 * 2**20
        ),
    )(part, exch, places)


def on_device(
    val_density, con_density, screened, coulomb, trans_here, trans_there, shift_map, ordering
):
    con = jnp.transpose(con_density, (1, 0, 2, 3)).reshape(KSEL, 36, 1024)
    val = jnp.transpose(val_density, (1, 0, 2, 3)).reshape(KSEL, NV, 1024)
    there = jnp.transpose(trans_there, (1, 0, 2, 3)).reshape(KSEL, NC, 1024)
    here = trans_here.reshape(NC, 1024)
    scr = screened.reshape(KSEL, 1024, 512)
    coul = jnp.concatenate([coulomb, coulomb], axis=1)
    within = (shift_map % GBLK).reshape(KSEL * 4, GBLK)
    part, exch = gather_and_multiply(con, val, here, scr, there, coul, within)
    cols = permute_and_sum(part, exch, ordering.reshape(1, NT))
    return jnp.transpose(cols.reshape(NC, KSEL, 2, NC), (1, 2, 3, 0))


def solution(mesh):
    in_specs = (
        P("pair", None, None, "ga"),
        P("ga", None, None, "pair"),
        P(None, None, "ga", "pair"),
        P(None, "ga"),
        P("pair", None, "ga"),
        P("pair", None, None, "ga"),
        P(None, "pair"),
        P(),
    )
    out_specs = P(None, None, "pair", "ga")
    return jax.shard_map(
        on_device, mesh=mesh, in_specs=in_specs, out_specs=out_specs, check_vma=False
    )
```

time: 405 us -> 125 us (0.31)
  the two profiles are of different devices: /device:TPU:2 before, /device:TPU:1 now
where the time goes in v2:
time: 125 us
  Pallas kernels  112 us (90%)
  local copies, waits for them, and re-layouts  10.1 us (8%)
  other arithmetic  2.08 us (2%)
    pallas_call x1, Pallas kernels, gather_and_multiply(): pl.pallas_call(tiles_kernel, name='gather_and_multiply', out_shape=(jax.S...  73.5 us
    pallas_call x1, Pallas kernels, permute_and_sum(): pl.pallas_call(order_kernel, name='permute_and_sum', out_shape=jax.ShapeD...  38.9 us
    unnamed x7, local copies, waits for them, and re-layouts  3.45 us

profile of v2, /device:TPU:1, one launch (start us, length us, event | category | flops | bytes accessed | tf_op | source)
XLA Modules:
  0.0 124.6 jit_solution(18155580585019942084)
XLA Ops:
  0.0 0.0 copy-start.2
  0.0 1.1 copy.9
  1.1 0.8 reshape.24.con_in
  1.9 1.0 copy.11
  2.9 0.7 reshape.28.there_ref
  3.7 1.0 copy.10
  4.7 0.7 reshape.25.val_in
  5.3 1.4 %copy.14 = bf16[3,8,2,512]{3,1,2,0:T(8,128)(2,1)} copy(bf16[3,8,2,512]{3,2,1,0:T(2,128)(2,1)} %bitcast.14) | data formatting | bytes 98304
  6.8 1.4 %pad_maximum_fusion.coul_ref = f32[3,1024]{1,0:T(4,128)} fusion(f32[3,512]{1,0:T(4,128)} %param.11), kind=kLoop, calls=%fused_computation | loop fusion | flops 3072 | bytes 18432 | tf_op jit(solution)/shard_map/concatenate | solution.py:488
  8.1 0.7 add_select_fusion
  8.8 0.6 reshape.29.within_ref
  9.5 73.5 %gather_and_multiply.1 = (f32[3,2,32,576]{3,2,1,0:T(8,128)}, f32[384,144]{1,0:T(8,128)}) custom-call(bf16[3,36,1024]{2,1,0:T(8,128)(2,1)} %reshape.24.con_in, bf16[3,16,1024]{2,1,0:T(8,128)(2,1)} %reshape.25.val_in, bf16[24,1024]{1,0:T(8,128)(2,1)} %bitcast.11, bf16[3,1024,512]{2,1,0:T(8,128)(2,1)} %bitcast.9, bf16[3,24,1024]{2,1,0:T(8,128)(2,1)} %reshape.28.there_ref, ...), custom_call_target="tpu_custom_call" | custom-call | tf_op jit(solution)/shard_map/gather_and_multiply/pallas_call | solution.py:305
  83.0 0.0 copy-done.2
  83.0 0.0 copy-start
  83.0 1.0 copy-done
  84.0 0.0 copy-start.1
  84.0 1.0 copy-done.1
  85.0 38.9 %permute_and_sum.1 = f32[24,144]{1,0:T(8,128)S(1)} custom-call(f32[3,2,32,576]{3,2,1,0:T(8,128)S(1)} %copy-done, f32[384,144]{1,0:T(8,128)S(1)} %copy-done.1, s32[1,384]{1,0:T(1,128)S(1)} %reshape.30.places_ref), custom_call_target="tpu_custom_call" | custom-call | tf_op jit(solution)/shard_map/permute_and_sum/pallas_call | solution.py:457
  123.9 0.7 copy.13
  (1 shorter events, 0.0 us)
Async XLA Ops:
  0.0 83.0 %copy-start.2 = (s32[384]{0:T(512)S(1)}, s32[384]{0:T(512)}, u32[]{:S(2)}) copy-start(s32[384]{0:T(512)} %param.15) | copy-start | bytes 4612
  83.0 1.0 copy-start
  84.0 1.0 copy-start.1

commit v3 on v1

v3 whole, which is shorter than its diff:
```python
import functools

import jax
import jax.numpy as jnp
from jax import lax
from jax.experimental import pallas as pl
from jax.experimental.pallas import tpu as pltpu
from jax.sharding import PartitionSpec as P

NV = 16
NC = 24
GBLK = 128
NT = 384
KSEL = 3
F32 = jnp.float32
BF16 = jnp.bfloat16
MESH = pl.DeviceIdType.MESH


def position():
    ga, pair = lax.axis_index("ga"), lax.axis_index("pair")
    return dict(
        ga=ga,
        pair=pair,
        zl=lax.div(ga, 4),
        y=lax.rem(ga, 4),
        zh=lax.div(pair, 8),
        x=lax.rem(lax.div(pair, 2), 4),
        core=lax.rem(pair, 2),
    )


def device(at, **moved):
    here = {**at, **moved}
    return (here["zl"] * 4 + here["y"], here["zh"] * 8 + here["x"] * 2 + here["core"])


def greet(peers):
    for peer in peers:
        pl.semaphore_signal(pltpu.get_barrier_semaphore(), inc=1, device_id=peer, device_id_type=MESH)


def remote(src, dst, send_sem, recv_sem, to):
    return pltpu.make_async_remote_copy(
        src_ref=src, dst_ref=dst, send_sem=send_sem, recv_sem=recv_sem, device_id=to, device_id_type=MESH
    )


def dot(left, right):
    return jnp.dot(left, right, preferred_element_type=F32)


def dot_rows(left, right):
    return lax.dot_general(left, right, (((1,), (1,)), ((), ())), preferred_element_type=F32)


def two_terms(values):
    high = values.astype(BF16)
    return high, (values - high.astype(F32)).astype(BF16)


def tiles_kernel(
    con_in, val_in, here_in, there_in, scr_in, coul_ref, shift_ref, places_ref,
    out_ref,
    con_raw, val_raw, here_raw, there_raw,
    con_all, val_all, here_all, here_rows, weights, con_rows, left_hi, left_lo, direct, from_core, from_x,
    rows_sel, cols_sel, exch_moved, parts, moved, from_rows, whole, cols, from_y, slab, from_z,
    con_send, con_recv, val_send, val_recv, here_send, here_recv,
    core_send, core_recv, x_send, x_recv, row_send, row_recv, y_send, y_recv, z_send, z_recv, local,
):
    at = position()
    ga, pair, zl, y, zh, x, core = (at[k] for k in ("ga", "pair", "zl", "y", "zh", "x", "core"))
    turn = lambda v, d: lax.rem(v + d, 4)
    other_core = device(at, core=1 - core)
    other_zh = device(at, zh=1 - zh)
    x_peers = [device(at, x=turn(x, d)) for d in (1, 2, 3)]
    y_peers = [device(at, y=turn(y, d)) for d in (1, 2, 3)]
    y_next, y_prev = y_peers[0], y_peers[2]
    row_steps = [(d, c) for c in (0, 1) for d in range(4) if (d, c) != (0, 0)]
    row_peers = [device(at, x=turn(x, d), core=lax.rem(core + c, 2)) for d, c in row_steps]
    z_to = [lax.rem(zh * 4 + zl + d, 8) for d in range(1, 8)]
    z_peers = [device(at, zh=lax.div(t, 4), zl=lax.rem(t, 4)) for t in z_to]

    loads = [
        pltpu.make_async_copy(src, dst, local.at[k])
        for k, (src, dst) in enumerate(
            [(val_in, val_raw), (con_in, con_raw), (here_in, here_raw), (there_in, there_raw)]
            + [(scr_in.at[q], weights.at[q]) for q in range(KSEL)]
        )
    ]
    for load in loads:
        load.start()
    greet(row_peers + y_peers + z_peers)
    loads[0].wait()
    for q in range(KSEL):
        for p in range(2):
            val_all[pair, q, :, p * 512 : (p + 1) * 512] = val_raw[:, q, p, :]
    loads[1].wait()
    for q in range(KSEL):
        for p in range(2):
            con_all[ga, q, p * 36 : (p + 1) * 36, :] = con_raw[:, q, p, :]
    loads[2].wait()
    for p in range(2):
        here_all[pair, :, p * 512 : (p + 1) * 512] = here_raw[:, p, :]
    pl.semaphore_wait(pltpu.get_barrier_semaphore(), len(row_peers + y_peers + z_peers))

    pending, maybe = [], []
    up, down = device(at, zl=turn(zl, 1)), device(at, zl=turn(zl, 3))

    def start(copy):
        copy.start()
        pending.append(copy)

    counts = {"con": 0, "val": 0, "here": 0}
    kinds = {"val": (val_all, val_send, val_recv), "here": (here_all, here_send, here_recv)}

    def send_pair(kind, owner, to):
        slots, send_sems, recv_sems = kinds[kind]
        start(remote(slots.at[owner], slots.at[owner], send_sems.at[counts[kind]], recv_sems.at[owner], to))
        counts[kind] += 1

    def wait_pair(kind, owner):
        slots, send_sems, recv_sems = kinds[kind]
        remote(slots.at[owner], slots.at[owner], send_sems.at[0], recv_sems.at[owner], other_core).wait_recv()

    def send_con(q, owner, to, when=None):
        slot = con_all.at[owner, q]
        copy = remote(slot, slot, con_send.at[counts["con"]], con_recv.at[owner, q], to)
        counts["con"] += 1
        if when is None:
            start(copy)
        else:
            pl.when(when)(copy.start)
            maybe.append((copy, when))

    def wait_con(q, owner):
        slot = con_all.at[owner, q]
        remote(slot, slot, con_send.at[0], con_recv.at[owner, q], other_core).wait_recv()

    def pair_at(zh_, x_, core_):
        return zh_ * 8 + x_ * 2 + core_

    def spread_own(kind):
        send_pair(kind, pair, other_zh)
        for peer in x_peers:
            send_pair(kind, pair, peer)
        send_pair(kind, pair, other_core)

    def spread_zh(kind):
        owner = pair_at(1 - zh, x, core)
        wait_pair(kind, owner)
        for peer in x_peers:
            send_pair(kind, owner, peer)
        send_pair(kind, owner, other_core)

    def spread_x(kind, zh_):
        for d in (1, 3, 2):
            owner = pair_at(zh_, turn(x, d), core)
            wait_pair(kind, owner)
            send_pair(kind, owner, other_core)

    def gather_rest(kind):
        for zh_ in (zh, 1 - zh):
            for d in (0, 1, 2, 3):
                wait_pair(kind, pair_at(zh_, turn(x, d), 1 - core))

    def con_z(q):
        send_con(q, ga, up, zl < 3)
        send_con(q, ga, down, zl > 0)

    def con_y(q):
        send_con(q, ga, y_next)
        send_con(q, ga, y_prev)

    def con_from_z(q, hops):
        for owner_zl, has, onward, goes in (
            (jnp.maximum(zl - hops, 0), zl >= hops, up, zl < 3),
            (jnp.minimum(zl + hops, 3), zl + hops <= 3, down, zl > 0),
        ):
            owner = owner_zl * 4 + y
            pl.when(has)(functools.partial(wait_con, q, owner))
            if hops < 3:
                send_con(q, owner, onward, jnp.logical_and(has, goes))
            send_con(q, owner, y_next, has)
            send_con(q, owner, y_prev, has)

    def con_from_y(q):
        for zl_ in (0, 1):
            owner = zl_ * 4 + turn(y, 3)
            wait_con(q, owner)
            send_con(q, owner, y_next)
        for zl_ in (2, 3):
            owner = zl_ * 4 + turn(y, 1)
            wait_con(q, owner)
            send_con(q, owner, y_prev)

    def con_rest(q):
        for zl_ in (2, 3):
            wait_con(q, zl_ * 4 + turn(y, 3))
        for zl_ in (0, 1):
            wait_con(q, zl_ * 4 + turn(y, 1))
        for zl_ in (0, 1, 2, 3):
            wait_con(q, zl_ * 4 + turn(y, 2))

    def unshift_weights(q):
        loads[4 + q].wait()
        for n in range(4):
            cols_ = slice(n * GBLK, (n + 1) * GBLK)
            row = shift_ref[pl.ds(q, 1), cols_] & (GBLK - 1)
            onehot = (lax.broadcasted_iota(jnp.int32, (GBLK, GBLK), 0) == row).astype(F32).astype(BF16)
            weights[q, :, cols_] = dot_rows(weights[q, :, cols_], onehot).astype(BF16)

    def rows_of(q):
        to_row = lax.broadcasted_iota(jnp.int32, (NV * NV, NV * NV), 0)
        from_row = lax.broadcasted_iota(jnp.int32, (NV * NV, NV * NV), 1)
        v, place = to_row & 15, to_row >> 4
        w = (place & 1) * 8 + ((place >> 1) & 3) * 2 + (place >> 3)
        order = (from_row == v * NV + w).astype(F32).astype(BF16)
        val = dot(order, val_all[:, q].reshape(NV * NV, 1024)).astype(BF16)
        val_re, val_im = val[:, :512], val[:, 512:]
        scr_re, scr_im = weights[q, :512, :], weights[q, 512:, :]
        real_hi, real_lo = two_terms(dot(val_re, scr_re) - dot(val_im, scr_im))
        imag_hi, imag_lo = two_terms(dot(val_re, scr_im) + dot(val_im, scr_re))
        for ref, real, imag in ((left_hi, real_hi, imag_hi), (left_lo, real_lo, imag_lo)):
            ref[q, 0, :, :512] = real
            ref[q, 0, :, 512:] = -imag
            ref[q, 1, :, :512] = imag
            ref[q, 1, :, 512:] = real

    def core_copy(q):
        other = pl.ds(pl.multiple_of((1 - core) * 128, 128), 128)
        return remote(direct.at[q, :, other, :], from_core.at[q], core_send.at[q], core_recv.at[q], other_core)

    def contract(q):
        con_rest(q)
        for owner in range(16):
            for p in range(2):
                con_rows[owner * 36 : (owner + 1) * 36, p * 512 : (p + 1) * 512] = con_all[
                    owner, q, p * 36 : (p + 1) * 36, :
                ]

        @pl.loop(0, 2)
        def _(p):
            direct[q, p] = dot_rows(left_hi[q, p], con_rows[...]) + dot_rows(left_lo[q, p], con_rows[...])

        start(core_copy(q))

    def x_copy(q, d):
        rows = pl.ds(pl.multiple_of(core * 128 + turn(x, d) * 32, 32), 32)
        return remote(
            direct.at[q, :, rows, :], from_x.at[q, d - 1], x_send.at[q, d - 1], x_recv.at[q, d - 1], x_peers[d - 1]
        )

    def add_core(q):
        core_copy(q).wait_recv()
        own = pl.ds(pl.multiple_of(core * 128, 128), 128)
        for p in range(2):
            direct[q, p, own, :] = direct[q, p, own, :] + from_core[q, p]
        for d in (2, 1, 3):
            start(x_copy(q, d))

    def row_copy(q, k):
        d, c = row_steps[k]
        rows = pl.ds(pl.multiple_of((turn(x, d) * 2 + lax.rem(core + c, 2)) * 48, 8), 48)
        return remote(
            moved.at[q, rows, :], from_rows.at[q, x * 2 + core], row_send.at[q, k], row_recv.at[q, x * 2 + core],
            row_peers[k],
        )

    def permute_rows(q):
        for d in (1, 2, 3):
            x_copy(q, d).wait_recv()
        for p in range(2):
            for half in range(2):
                rows = pl.ds(pl.multiple_of(core * 128 + x * 32 + half * NV, 16), NV)
                block = slice(half * NV, (half + 1) * NV)
                tile = direct[q, p, rows, :] + from_x[q, 0, p, block] + from_x[q, 1, p, block] + from_x[q, 2, p, block]
                lane = half * 48 + p * NC
                for c in range(NC):
                    parts[c * NV : (c + 1) * NV, lane : lane + NC] = tile[:, c * NC : (c + 1) * NC]
        high, low = two_terms(parts[...])
        moved[q] = exch_moved[q] - dot(rows_sel[...], high) - dot(rows_sel[...], low)
        for k in (1, 0, 2, 5, 4, 6, 3):
            start(row_copy(q, k))
        from_rows[q, x * 2 + core] = moved[q, pl.ds(pl.multiple_of((x * 2 + core) * 48, 8), 48), :]

    def y_copy(q, d):
        rows = pl.ds(pl.multiple_of(turn(y, d) * 96, 32), 96)
        return remote(
            cols.at[q, rows, :], from_y.at[q, d - 1], y_send.at[q, d - 1], y_recv.at[q, d - 1], y_peers[d - 1]
        )

    def permute_cols(q):
        for k, (d, c) in enumerate(row_steps):
            slot = from_rows.at[q, turn(x, d) * 2 + lax.rem(core + c, 2)]
            recv = row_recv.at[q, turn(x, d) * 2 + lax.rem(core + c, 2)]
            remote(slot, slot, row_send.at[q, k], recv, row_peers[k]).wait_recv()
        for slot in range(8):
            for half in range(2):
                tile = from_rows[q, slot, half * NC : (half + 1) * NC, :]
                for zh_ in range(2):
                    w = zh_ * 8 + slot
                    for p in range(2):
                        lane, row = zh_ * 48 + p * NC, half * 48 + p * NC
                        whole[row : row + NC, w * NC : (w + 1) * NC] = tile[:, lane : lane + NC]
        high, low = two_terms(whole[...])
        cols[q] = dot_rows(cols_sel[...], high) + dot_rows(cols_sel[...], low)
        for d in (2, 1, 3):
            start(y_copy(q, d))

    def z_copy(q, d):
        rows = pl.ds(pl.multiple_of(lax.rem(z_to[d - 1], 4) * NC, 8), NC)
        return remote(
            slab.at[q, rows, :], from_z.at[q, d - 1], z_send.at[q, d - 1], z_recv.at[q, d - 1], z_peers[d - 1]
        )

    def add_y(q):
        for d in (1, 2, 3):
            y_copy(q, d).wait_recv()
        own = pl.ds(pl.multiple_of(y * 96, 32), 96)
        slab[q] = cols[q, own, :] + from_y[q, 0] + from_y[q, 1] + from_y[q, 2]
        for d in (4, 3, 5, 2, 6, 1, 7):
            start(z_copy(q, d))

    def add_z(q):
        total = slab[q, pl.ds(pl.multiple_of(zl * NC, 8), NC), :]
        for d in range(1, 8):
            z_copy(q, d).wait_recv()
        for d in range(7):
            total = total + from_z[q, d]
        out_ref[q] = jnp.where(zh == 0, total[:, :48], total[:, 48:])

    def select():
        places = jnp.transpose(jnp.broadcast_to(places_ref[...].astype(F32), (GBLK, NT))).astype(jnp.int32)
        lanes = lax.broadcasted_iota(jnp.int32, (NT, GBLK), 1)

        def block(k):
            return places[k * NC : (k + 1) * NC]

        by_rows = jnp.concatenate([block(zh_ * 8 + s) for s in range(8) for zh_ in range(2)], axis=0)
        by_cols = jnp.concatenate([block(zl_ * 4 + y_) for y_ in range(4) for zl_ in range(4)], axis=0)
        band = jnp.zeros((NT, GBLK), jnp.int32)
        for step in range(1, NV):
            band = band + (by_rows >= step * NC).astype(jnp.int32)
        swapped = (by_rows - band * NC) * NV + band

        def onehot(which):
            parts_ = [(which == lanes + n * GBLK).astype(F32) for n in range(3)]
            return jnp.concatenate(parts_, axis=1).astype(BF16)

        rows_sel[...] = onehot(swapped)
        cols_sel[...] = onehot(by_cols)
        return onehot(by_rows)

    def exchange():
        by_rows = select()
        gather_rest("here")
        for v in range(NV):
            here_rows[v * NC : (v + 1) * NC, :] = here_all[v]
        loads[3].wait()
        highs, lows = [], []
        for q in range(KSEL):
            coul = coul_ref[pl.ds(q, 1), :]
            real_hi, real_lo = two_terms(there_raw[:, q, 0, :].astype(F32) * coul)
            imag_hi, imag_lo = two_terms(there_raw[:, q, 1, :].astype(F32) * coul)
            for out, real, imag in ((highs, real_hi, imag_hi), (lows, real_lo, imag_lo)):
                real, imag = real.astype(F32), imag.astype(F32)
                out.append(jnp.concatenate([real, -imag], axis=1))
                out.append(jnp.concatenate([imag, real], axis=1))
        highs = jnp.concatenate(highs, axis=0).astype(BF16)
        lows = jnp.concatenate(lows, axis=0).astype(BF16)
        high, low = two_terms(dot_rows(here_rows[...], highs) + dot_rows(here_rows[...], lows))
        ordered = 2.0 * (dot(by_rows, high) + dot(by_rows, low))
        for q in range(KSEL):
            tile = ordered[:, q * 48 : (q + 1) * 48]
            exch_moved[q, :, 0:48] = jnp.where(zh == 0, tile, 0.0)
            exch_moved[q, :, 48:96] = jnp.where(zh == 1, tile, 0.0)

    spread_own("val")
    for q in range(KSEL):
        con_z(q)
        con_y(q)
    for q in range(KSEL):
        unshift_weights(q)
    con_from_z(0, 1)
    spread_zh("val")
    spread_x("val", zh)
    con_from_z(1, 1)
    con_from_z(0, 2)
    spread_x("val", 1 - zh)
    con_from_z(2, 1)
    con_from_z(1, 2)
    con_from_z(0, 3)
    gather_rest("val")
    rows_of(0)
    con_from_y(0)
    con_from_z(2, 2)
    con_from_z(1, 3)
    spread_own("here")
    rows_of(1)
    contract(0)
    con_from_z(2, 3)
    con_from_y(1)
    rows_of(2)
    spread_zh("here")
    add_core(0)
    spread_x("here", zh)
    contract(1)
    con_from_y(2)
    spread_x("here", 1 - zh)
    add_core(1)
    exchange()
    permute_rows(0)
    permute_cols(0)
    contract(2)
    permute_rows(1)
    add_core(2)
    add_y(0)
    permute_cols(1)
    permute_rows(2)
    add_y(1)
    permute_cols(2)
    add_y(2)
    for q in range(KSEL):
        add_z(q)
    for copy, when in maybe:
        pl.when(when)(copy.wait_send)
    for copy in pending:
        copy.wait_send()


def kernel_tiles(con, val, here, there, scr, coul, shift, places):
    any_space = pl.BlockSpec(memory_space=pl.ANY)
    vmem = pl.BlockSpec(memory_space=pltpu.VMEM)
    dma = pltpu.SemaphoreType.DMA
    return pl.pallas_call(
        tiles_kernel,
        name="kernel_tiles",
        out_shape=jax.ShapeDtypeStruct((KSEL, NC, 2 * NC), F32),
        in_specs=[any_space] * 5 + [vmem] * 3,
        out_specs=vmem,
        scratch_shapes=[
            pltpu.VMEM(con.shape, BF16),
            pltpu.VMEM(val.shape, BF16),
            pltpu.VMEM(here.shape, BF16),
            pltpu.VMEM(there.shape, BF16),
            pltpu.VMEM((16, KSEL, 72, 512), BF16),
            pltpu.VMEM((16, KSEL, NV, 1024), BF16),
            pltpu.VMEM((16, NC, 1024), BF16),
            pltpu.VMEM((NT, 1024), BF16),
            pltpu.VMEM((KSEL, 1024, 512), BF16),
            pltpu.VMEM((NC * NC, 1024), BF16),
            pltpu.VMEM((KSEL, 2, NV * NV, 1024), BF16),
            pltpu.VMEM((KSEL, 2, NV * NV, 1024), BF16),
            pltpu.VMEM((KSEL, 2, NV * NV, NC * NC), F32),
            pltpu.VMEM((KSEL, 2, 128, NC * NC), F32),
            pltpu.VMEM((KSEL, 3, 2, 32, NC * NC), F32),
            pltpu.VMEM((NT, NT), BF16),
            pltpu.VMEM((NT, NT), BF16),
            pltpu.VMEM((KSEL, NT, 96), F32),
            pltpu.VMEM((NT, 96), F32),
            pltpu.VMEM((KSEL, NT, 96), F32),
            pltpu.VMEM((KSEL, 8, 48, 96), F32),
            pltpu.VMEM((96, NT), F32),
            pltpu.VMEM((KSEL, NT, 96), F32),
            pltpu.VMEM((KSEL, 3, 96, 96), F32),
            pltpu.VMEM((KSEL, 96, 96), F32),
            pltpu.VMEM((KSEL, 7, NC, 96), F32),
            dma((72,)), dma((16, KSEL)), dma((16,)), dma((16,)), dma((16,)), dma((16,)),
            dma((KSEL,)), dma((KSEL,)), dma((KSEL, 3)), dma((KSEL, 3)), dma((KSEL, 7)), dma((KSEL, 8)),
            dma((KSEL, 3)), dma((KSEL, 3)), dma((KSEL, 7)), dma((KSEL, 7)), dma((7,)),
        ],
        compiler_params=pltpu.CompilerParams(
            collective_id=0, has_side_effects=True, vmem_limit_bytes=60 * 2**20
        ),
    )(con, val, here, there, scr, coul, shift, places)


def on_device(
    val_density, con_density, screened, coulomb, trans_here, trans_there, shift_map, ordering
):
    tiles = kernel_tiles(
        con_density, val_density, trans_here, trans_there, screened.reshape(KSEL, 1024, 512),
        coulomb, shift_map, ordering.reshape(1, NT),
    )
    return jnp.transpose(tiles.reshape(KSEL, NC, 2, NC), (0, 2, 3, 1))


def solution(mesh):
    in_specs = (
        P("pair", None, None, "ga"),
        P("ga", None, None, "pair"),
        P(None, None, "ga", "pair"),
        P(None, "ga"),
        P("pair", None, "ga"),
        P("pair", None, None, "ga"),
        P(None, "pair"),
        P(),
    )
    out_specs = P(None, None, "pair", "ga")
    return jax.shard_map(
        on_device, mesh=mesh, in_specs=in_specs, out_specs=out_specs, check_vma=False
    )
```

time: 405 us -> 95.8 us (0.24)
  the two profiles are of different devices: /device:TPU:2 before, /device:TPU:1 now
where the time goes in v3:
time: 95.8 us; the launch traced here: 95.6 us
  Pallas kernels  92.8 us (97%)
  local copies, waits for them, and re-layouts  2.74 us (3%)
    pallas_call x1, Pallas kernels, kernel_tiles(): pl.pallas_call(tiles_kernel, name='kernel_tiles', out_shape=jax.ShapeDtyp...  92.8 us

profile of v3, /device:TPU:1, one launch (start us, length us, event | category | flops | bytes accessed | tf_op | source)
XLA Modules:
  0.0 95.6 jit_solution(5908838633323584990)
XLA Ops:
  0.0 1.2 %reshape.10.places_ref = s32[1,384]{1,0:T(1,128)} reshape(s32[384]{0:T(512)} %param.15) | data formatting | bytes 3072 | tf_op jit(solution)/shard_map/reshape | solution.py:484
  1.2 92.8 %kernel_tiles.1 = f32[3,24,48]{2,1,0:T(8,128)} custom-call(bf16[36,3,2,512]{3,2,1,0:T(2,128)(2,1)} %con_in.1, bf16[16,3,2,512]{3,2,1,0:T(2,128)(2,1)} %val_in.1, bf16[24,2,512]{2,1,0:T(2,128)(2,1)} %here_in.1, bf16[24,3,2,512]{3,2,1,0:T(2,128)(2,1)} %there_in.1, bf16[3,1024,512]{2,1,0:T(8,128)(2,1)} %bitcast.4, f32[3,512]{1,0:T(4,128)} %coul_ref.1, ...), custom_call_target="tpu_custom_call" | custom-call | tf_op jit(solution)/shard_map/kernel_tiles/pallas_call | solution.py:436
  94.1 1.5 %copy.10 = f32[3,24,48]{1,2,0:T(8,128)} copy(f32[3,24,48]{2,1,0:T(8,128)} %kernel_tiles.1) | data formatting | bytes 27648 | tf_op jit(solution)/shard_map/reshape | solution.py:486

commit v4 on v3

--- a/solution.py
+++ b/solution.py
@@ -94,7 +94,7 @@
     loads[0].wait()
     for q in range(KSEL):
         for p in range(2):
-            val_all[pair, q, :, p * 512 : (p + 1) * 512] = val_raw[:, q, p, :]
+            val_all[q, pair, :, p * 512 : (p + 1) * 512] = val_raw[:, q, p, :]
     loads[1].wait()
     for q in range(KSEL):
         for p in range(2):
@@ -111,8 +111,9 @@
         copy.start()
         pending.append(copy)
 
-    counts = {"con": 0, "val": 0, "here": 0}
-    kinds = {"val": (val_all, val_send, val_recv), "here": (here_all, here_send, here_recv)}
+    kinds = {q: (val_all.at[q], val_send.at[q], val_recv.at[q]) for q in range(KSEL)}
+    kinds["here"] = (here_all, here_send, here_recv)
+    counts = dict.fromkeys(["con", *kinds], 0)
 
     def send_pair(kind, owner, to):
         slots, send_sems, recv_sems = kinds[kind]
@@ -167,6 +168,19 @@
     def con_z(q):
         send_con(q, ga, up, zl < 3)
         send_con(q, ga, down, zl > 0)
+
+    near, far = jnp.maximum(zl - 1, 1 - zl), 3 - 3 * lax.div(zl, 2)
+    line = (near, 6 - zl - near - far, far)
+
+    def con_line(q):
+        for zl_ in line:
+            send_con(q, ga, device(at, zl=zl_))
+
+    def con_from_line(q, k):
+        owner = line[k] * 4 + y
+        wait_con(q, owner)
+        send_con(q, owner, y_next)
+        send_con(q, owner, y_prev)
 
     def con_y(q):
         send_con(q, ga, y_next)
@@ -216,7 +230,7 @@
         v, place = to_row & 15, to_row >> 4
         w = (place & 1) * 8 + ((place >> 1) & 3) * 2 + (place >> 3)
         order = (from_row == v * NV + w).astype(F32).astype(BF16)
-        val = dot(order, val_all[:, q].reshape(NV * NV, 1024)).astype(BF16)
+        val = dot(order, val_all[q].reshape(NV * NV, 1024)).astype(BF16)
         val_re, val_im = val[:, :512], val[:, 512:]
         scr_re, scr_im = weights[q, :512, :], weights[q, 512:, :]
         real_hi, real_lo = two_terms(dot(val_re, scr_re) - dot(val_im, scr_im))
@@ -227,9 +241,11 @@
             ref[q, 1, :, :512] = imag
             ref[q, 1, :, 512:] = real
 
-    def core_copy(q):
+    def core_copy(q, p):
         other = pl.ds(pl.multiple_of((1 - core) * 128, 128), 128)
-        return remote(direct.at[q, :, other, :], from_core.at[q], core_send.at[q], core_recv.at[q], other_core)
+        return remote(
+            direct.at[q, p, other, :], from_core.at[q, p], core_send.at[q, p], core_recv.at[q, p], other_core
+        )
 
     def contract(q):
         con_rest(q)
@@ -238,26 +254,46 @@
                 con_rows[owner * 36 : (owner + 1) * 36, p * 512 : (p + 1) * 512] = con_all[
                     owner, q, p * 36 : (p + 1) * 36, :
                 ]
-
-        @pl.loop(0, 2)
-        def _(p):
+        for p in range(2):
             direct[q, p] = dot_rows(left_hi[q, p], con_rows[...]) + dot_rows(left_lo[q, p], con_rows[...])
-
-        start(core_copy(q))
-
-    def x_copy(q, d):
-        rows = pl.ds(pl.multiple_of(core * 128 + turn(x, d) * 32, 32), 32)
+            start(core_copy(q, p))
+
+    def x_copy(q, p, slot, rows_for, to):
+        rows = pl.ds(pl.multiple_of(core * 128 + turn(x, rows_for) * 32, 32), 32)
         return remote(
-            direct.at[q, :, rows, :], from_x.at[q, d - 1], x_send.at[q, d - 1], x_recv.at[q, d - 1], x_peers[d - 1]
+            direct.at[q, p, rows, :], from_x.at[q, slot, p],
+            x_send.at[q, p, slot], x_recv.at[q, p, slot], x_peers[to - 1],
         )
 
+    def to_each(q, p, d):
+        return x_copy(q, p, d - 1, d, d)
+
+    def to_side(q, p, side):
+        return x_copy(q, p, side, 3 if side else 1, 3 if side else 1)
+
+    def by_side(q, p):
+        return x_copy(q, p, 2, 2, 3 if p else 1)
+
     def add_core(q):
-        core_copy(q).wait_recv()
         own = pl.ds(pl.multiple_of(core * 128, 128), 128)
         for p in range(2):
+            core_copy(q, p).wait_recv()
             direct[q, p, own, :] = direct[q, p, own, :] + from_core[q, p]
-        for d in (2, 1, 3):
-            start(x_copy(q, d))
+            if q == 2:
+                for d in (2, 1, 3):
+                    start(to_each(q, p, d))
+            else:
+                start(by_side(q, p))
+        if q < 2:
+            for p in range(2):
+                start(to_side(q, p, 1 - p))
+
+    def relay(q):
+        for p in range(2):
+            by_side(q, p).wait_recv()
+            rows = pl.ds(pl.multiple_of(core * 128 + turn(x, 3 if p else 1) * 32, 32), 32)
+            direct[q, p, rows, :] = direct[q, p, rows, :] + from_x[q, 2, p]
+            start(to_side(q, p, p))
 
     def row_copy(q, k):
         d, c = row_steps[k]
@@ -268,13 +304,15 @@
         )
 
     def permute_rows(q):
-        for d in (1, 2, 3):
-            x_copy(q, d).wait_recv()
         for p in range(2):
+            for copy in [to_each(q, p, d) for d in (1, 2, 3)] if q == 2 else [to_side(q, p, k) for k in (0, 1)]:
+                copy.wait_recv()
             for half in range(2):
                 rows = pl.ds(pl.multiple_of(core * 128 + x * 32 + half * NV, 16), NV)
                 block = slice(half * NV, (half + 1) * NV)
-                tile = direct[q, p, rows, :] + from_x[q, 0, p, block] + from_x[q, 1, p, block] + from_x[q, 2, p, block]
+                tile = direct[q, p, rows, :] + from_x[q, 0, p, block] + from_x[q, 1, p, block]
+                if q == 2:
+                    tile = tile + from_x[q, 2, p, block]
                 lane = half * 48 + p * NC
                 for c in range(NC):
                     parts[c * NV : (c + 1) * NV, lane : lane + NC] = tile[:, c * NC : (c + 1) * NC]
@@ -328,10 +366,10 @@
             z_copy(q, d).wait_recv()
         for d in range(7):
             total = total + from_z[q, d]
-        out_ref[q] = jnp.where(zh == 0, total[:, :48], total[:, 48:])
+        out_ref[:, q * 48 : (q + 1) * 48] = jnp.where(zh == 0, total[:, :48], total[:, 48:])
 
     def select():
-        places = jnp.transpose(jnp.broadcast_to(places_ref[...].astype(F32), (GBLK, NT))).astype(jnp.int32)
+        places = jnp.transpose(jnp.broadcast_to(places_ref[...].astype(F32)[None, :], (GBLK, NT))).astype(jnp.int32)
         lanes = lax.broadcasted_iota(jnp.int32, (NT, GBLK), 1)
 
         def block(k):
@@ -376,53 +414,70 @@
             exch_moved[q, :, 0:48] = jnp.where(zh == 0, tile, 0.0)
             exch_moved[q, :, 48:96] = jnp.where(zh == 1, tile, 0.0)
 
-    spread_own("val")
-    for q in range(KSEL):
-        con_z(q)
-        con_y(q)
-    for q in range(KSEL):
-        unshift_weights(q)
-    con_from_z(0, 1)
-    spread_zh("val")
-    spread_x("val", zh)
+    spread_own(0)
+    con_line(0)
+    con_y(0)
+    con_y(1)
+    con_y(2)
+    unshift_weights(0)
+    con_from_line(0, 0)
+    con_z(1)
+    spread_zh(0)
+    con_from_line(0, 1)
+    spread_own(1)
+    spread_x(0, zh)
+    con_from_line(0, 2)
+    con_z(2)
+    spread_own(2)
+    spread_x(0, 1 - zh)
     con_from_z(1, 1)
-    con_from_z(0, 2)
-    spread_x("val", 1 - zh)
-    con_from_z(2, 1)
-    con_from_z(1, 2)
-    con_from_z(0, 3)
-    gather_rest("val")
+    spread_own("here")
+    gather_rest(0)
     rows_of(0)
     con_from_y(0)
+    spread_zh(1)
+    con_from_z(1, 2)
+    con_from_z(2, 1)
+    spread_x(1, zh)
+    spread_zh(2)
+    spread_x(1, 1 - zh)
+    con_from_z(1, 3)
+    spread_x(2, zh)
+    spread_zh("here")
+    contract(0)
+    con_from_y(1)
     con_from_z(2, 2)
-    con_from_z(1, 3)
-    spread_own("here")
+    add_core(0)
+    spread_x(2, 1 - zh)
+    spread_x("here", zh)
+    con_from_z(2, 3)
+    unshift_weights(1)
+    unshift_weights(2)
+    spread_x("here", 1 - zh)
+    gather_rest(1)
     rows_of(1)
-    contract(0)
-    con_from_z(2, 3)
-    con_from_y(1)
+    gather_rest(2)
     rows_of(2)
-    spread_zh("here")
-    add_core(0)
-    spread_x("here", zh)
+    exchange()
+    relay(0)
+    con_from_y(2)
     contract(1)
-    con_from_y(2)
-    spread_x("here", 1 - zh)
     add_core(1)
-    exchange()
     permute_rows(0)
+    contract(2)
+    relay(1)
+    add_core(2)
+    permute_rows(1)
     permute_cols(0)
-    contract(2)
-    permute_rows(1)
-    add_core(2)
+    permute_rows(2)
     add_y(0)
     permute_cols(1)
-    permute_rows(2)
+    permute_cols(2)
     add_y(1)
-    permute_cols(2)
+    add_z(0)
     add_y(2)
-    for q in range(KSEL):
-        add_z(q)
+    add_z(1)
+    add_z(2)
     for copy, when in maybe:
         pl.when(when)(copy.wait_send)
     for copy in pending:
@@ -436,7 +491,7 @@
     return pl.pallas_call(
         tiles_kernel,
         name="kernel_tiles",
-        out_shape=jax.ShapeDtypeStruct((KSEL, NC, 2 * NC), F32),
+        out_shape=jax.ShapeDtypeStruct((NC, KSEL * 2 * NC), F32),
         in_specs=[any_space] * 5 + [vmem] * 3,
         out_specs=vmem,
         scratch_shapes=[
@@ -445,7 +500,7 @@
             pltpu.VMEM(here.shape, BF16),
             pltpu.VMEM(there.shape, BF16),
             pltpu.VMEM((16, KSEL, 72, 512), BF16),
-            pltpu.VMEM((16, KSEL, NV, 1024), BF16),
+            pltpu.VMEM((KSEL, 16, NV, 1024), BF16),
             pltpu.VMEM((16, NC, 1024), BF16),
             pltpu.VMEM((NT, 1024), BF16),
             pltpu.VMEM((KSEL, 1024, 512), BF16),
@@ -466,8 +521,8 @@
             pltpu.VMEM((KSEL, 3, 96, 96), F32),
             pltpu.VMEM((KSEL, 96, 96), F32),
             pltpu.VMEM((KSEL, 7, NC, 96), F32),
-            dma((72,)), dma((16, KSEL)), dma((16,)), dma((16,)), dma((16,)), dma((16,)),
-            dma((KSEL,)), dma((KSEL,)), dma((KSEL, 3)), dma((KSEL, 3)), dma((KSEL, 7)), dma((KSEL, 8)),
+            dma((72,)), dma((16, KSEL)), dma((KSEL, 16)), dma((KSEL, 16)), dma((16,)), dma((16,)),
+            dma((KSEL, 2)), dma((KSEL, 2)), dma((KSEL, 2, 3)), dma((KSEL, 2, 3)), dma((KSEL, 7)), dma((KSEL, 8)),
             dma((KSEL, 3)), dma((KSEL, 3)), dma((KSEL, 7)), dma((KSEL, 7)), dma((7,)),
         ],
         compiler_params=pltpu.CompilerParams(
@@ -481,9 +536,9 @@
 ):
     tiles = kernel_tiles(
         con_density, val_density, trans_here, trans_there, screened.reshape(KSEL, 1024, 512),
-        coulomb, shift_map, ordering.reshape(1, NT),
+        coulomb, shift_map, ordering,
     )
-    return jnp.transpose(tiles.reshape(KSEL, NC, 2, NC), (0, 2, 3, 1))
+    return jnp.transpose(tiles.reshape(NC, KSEL, 2, NC), (1, 2, 3, 0))
 
 
 def solution(mesh):

time: 95.8 us -> 83.9 us (0.88)
  Pallas kernels: 92.8 us -> 82.2 us
  local copies, waits for them, and re-layouts: 2.74 us -> 1.47 us
    pallas_call x1, Pallas kernels: 92.8 us -> 82.2 us  [kernel_tiles(): pl.pallas_call(tiles_kernel, name='kernel_tiles', out_shape=jax.ShapeDtyp...]
    reshape x2 -> x1, local copies, waits for them, and re-layouts: 2.74 us -> 1.47 us  [on_device(): return jnp.transpose(tiles.reshape(NC, KSEL, 2, NC), (1, 2, 3, 0))]
where the time goes in v4:
time: 83.9 us; the launch traced here: 83.7 us
  Pallas kernels  82.2 us (98%)
  local copies, waits for them, and re-layouts  1.47 us (2%)
    pallas_call x1, Pallas kernels, kernel_tiles(): pl.pallas_call(tiles_kernel, name='kernel_tiles', out_shape=jax.ShapeDtyp...  82.2 us

profile of v4, /device:TPU:1, one launch (start us, length us, event | category | flops | bytes accessed | tf_op | source)
XLA Modules:
  0.0 83.7 jit_solution(5254164112177833961)
XLA Ops:
  0.0 82.2 %kernel_tiles.1 = f32[24,144]{1,0:T(8,128)} custom-call(bf16[36,3,2,512]{3,2,1,0:T(2,128)(2,1)} %con_in.1, bf16[16,3,2,512]{3,2,1,0:T(2,128)(2,1)} %val_in.1, bf16[24,2,512]{2,1,0:T(2,128)(2,1)} %here_in.1, bf16[24,3,2,512]{3,2,1,0:T(2,128)(2,1)} %there_in.1, bf16[3,1024,512]{2,1,0:T(8,128)(2,1)} %bitcast.4, f32[3,512]{1,0:T(4,128)} %coul_ref.1, ...), custom_call_target="tpu_custom_call" | custom-call | tf_op jit(solution)/shard_map/kernel_tiles/pallas_call | solution.py:491
  82.2 1.5 %copy.10 = f32[24,144]{0,1:T(8,128)} copy(f32[24,144]{1,0:T(8,128)} %kernel_tiles.1) | data formatting | bytes 27648 | tf_op jit(solution)/shard_map/reshape | solution.py:541

commit v5 on v4

--- a/solution.py
+++ b/solution.py
@@ -265,9 +265,6 @@
             x_send.at[q, p, slot], x_recv.at[q, p, slot], x_peers[to - 1],
         )
 
-    def to_each(q, p, d):
-        return x_copy(q, p, d - 1, d, d)
-
     def to_side(q, p, side):
         return x_copy(q, p, side, 3 if side else 1, 3 if side else 1)
 
@@ -279,14 +276,9 @@
         for p in range(2):
             core_copy(q, p).wait_recv()
             direct[q, p, own, :] = direct[q, p, own, :] + from_core[q, p]
-            if q == 2:
-                for d in (2, 1, 3):
-                    start(to_each(q, p, d))
-            else:
-                start(by_side(q, p))
-        if q < 2:
-            for p in range(2):
-                start(to_side(q, p, 1 - p))
+            start(by_side(q, p))
+        for p in range(2):
+            start(to_side(q, p, 1 - p))
 
     def relay(q):
         for p in range(2):
@@ -305,14 +297,12 @@
 
     def permute_rows(q):
         for p in range(2):
-            for copy in [to_each(q, p, d) for d in (1, 2, 3)] if q == 2 else [to_side(q, p, k) for k in (0, 1)]:
+            for copy in [to_side(q, p, k) for k in (0, 1)]:
                 copy.wait_recv()
             for half in range(2):
                 rows = pl.ds(pl.multiple_of(core * 128 + x * 32 + half * NV, 16), NV)
                 block = slice(half * NV, (half + 1) * NV)
                 tile = direct[q, p, rows, :] + from_x[q, 0, p, block] + from_x[q, 1, p, block]
-                if q == 2:
-                    tile = tile + from_x[q, 2, p, block]
                 lane = half * 48 + p * NC
                 for c in range(NC):
                     parts[c * NV : (c + 1) * NV, lane : lane + NC] = tile[:, c * NC : (c + 1) * NC]
@@ -416,12 +406,12 @@
 
     spread_own(0)
     con_line(0)
+    con_z(1)
     con_y(0)
     con_y(1)
     con_y(2)
     unshift_weights(0)
     con_from_line(0, 0)
-    con_z(1)
     spread_zh(0)
     con_from_line(0, 1)
     spread_own(1)
@@ -467,8 +457,9 @@
     contract(2)
     relay(1)
     add_core(2)
+    permute_cols(0)
+    relay(2)
     permute_rows(1)
-    permute_cols(0)
     permute_rows(2)
     add_y(0)
     permute_cols(1)

time: 83.9 us -> 82.3 us (0.981)
  Pallas kernels: 82.2 us -> 80.7 us
    pallas_call x1, Pallas kernels: 82.2 us -> 80.7 us  [kernel_tiles(): pl.pallas_call(tiles_kernel, name='kernel_tiles', out_shape=jax.ShapeDtyp...]
where the time goes in v5:
time: 82.3 us; the launch traced here: 82.2 us
  Pallas kernels  80.7 us (98%)
  local copies, waits for them, and re-layouts  1.47 us (2%)
    pallas_call x1, Pallas kernels, kernel_tiles(): pl.pallas_call(tiles_kernel, name='kernel_tiles', out_shape=jax.ShapeDtyp...  80.7 us

profile of v5, /device:TPU:1, one launch (start us, length us, event | category | flops | bytes accessed | tf_op | source)
XLA Modules:
  0.0 82.2 jit_solution(8446065147335774389)
XLA Ops:
  0.0 80.7 %kernel_tiles.1 = f32[24,144]{1,0:T(8,128)} custom-call(bf16[36,3,2,512]{3,2,1,0:T(2,128)(2,1)} %con_in.1, bf16[16,3,2,512]{3,2,1,0:T(2,128)(2,1)} %val_in.1, bf16[24,2,512]{2,1,0:T(2,128)(2,1)} %here_in.1, bf16[24,3,2,512]{3,2,1,0:T(2,128)(2,1)} %there_in.1, bf16[3,1024,512]{2,1,0:T(8,128)(2,1)} %bitcast.4, f32[3,512]{1,0:T(4,128)} %coul_ref.1, ...), custom_call_target="tpu_custom_call" | custom-call | tf_op jit(solution)/shard_map/kernel_tiles/pallas_call | solution.py:482
  80.7 1.5 %copy.10 = f32[24,144]{0,1:T(8,128)} copy(f32[24,144]{1,0:T(8,128)} %kernel_tiles.1) | data formatting | bytes 27648 | tf_op jit(solution)/shard_map/reshape | solution.py:532

commit v6 on v5

--- a/solution.py
+++ b/solution.py
@@ -414,10 +414,10 @@
     con_from_line(0, 0)
     spread_zh(0)
     con_from_line(0, 1)
+    con_z(2)
     spread_own(1)
     spread_x(0, zh)
     con_from_line(0, 2)
-    con_z(2)
     spread_own(2)
     spread_x(0, 1 - zh)
     con_from_z(1, 1)

time: 82.3 us -> 82.6 us (level)
  no operation moved by 1% of the time
where the time goes in v6:
time: 82.6 us; the launch traced here: 82.4 us
  Pallas kernels  80.9 us (98%)
  local copies, waits for them, and re-layouts  1.47 us (2%)
    pallas_call x1, Pallas kernels, kernel_tiles(): pl.pallas_call(tiles_kernel, name='kernel_tiles', out_shape=jax.ShapeDtyp...  80.9 us

profile of v6, /device:TPU:1, one launch (start us, length us, event | category | flops | bytes accessed | tf_op | source)
XLA Modules:
  0.0 82.4 jit_solution(11323722178756266768)
XLA Ops:
  0.0 80.9 %kernel_tiles.1 = f32[24,144]{1,0:T(8,128)} custom-call(bf16[36,3,2,512]{3,2,1,0:T(2,128)(2,1)} %con_in.1, bf16[16,3,2,512]{3,2,1,0:T(2,128)(2,1)} %val_in.1, bf16[24,2,512]{2,1,0:T(2,128)(2,1)} %here_in.1, bf16[24,3,2,512]{3,2,1,0:T(2,128)(2,1)} %there_in.1, bf16[3,1024,512]{2,1,0:T(8,128)(2,1)} %bitcast.4, f32[3,512]{1,0:T(4,128)} %coul_ref.1, ...), custom_call_target="tpu_custom_call" | custom-call | tf_op jit(solution)/shard_map/kernel_tiles/pallas_call | solution.py:482
  80.9 1.5 %copy.10 = f32[24,144]{0,1:T(8,128)} copy(f32[24,144]{1,0:T(8,128)} %kernel_tiles.1) | data formatting | bytes 27648 | tf_op jit(solution)/shard_map/reshape | solution.py:532
